TPU v7x, 256 devices: a whole 4x4x8 slice. The times are simulated.
256 devices in a mesh: sub: 64 (over z, y, core), rhs: 4 (over x).
Axes of the slice: x: 4, y: 4, z: 8, core: 2. Of those that a mesh axis runs over, the one named last changes fastest.
Arguments:
- stiffness: float32 [3072, 4, 9216], P('sub'), may hold values from -1 to 2, as said below
- precond: float32 [3072, 9216], P('sub'), may hold values from -0.625 to 0.625
- rhs_vec: float32 [8, 294912], P('rhs', 'sub'), may hold values from -50 to 50
- cotangent: float32 [8, 294912], P('rhs', 'sub'), may hold values from -6 to 6
- col_index: int32 [3072, 4], P('sub'), may hold values from 0 to 59, as said below
- send_rows: int32 [64, 12], P('sub'), may hold values from 0 to 47, as said below
- counts: int32 [64], P('sub'), may hold values from 12 to 48, as said below
Outputs:
- solution: float32 [8, 294912], P('rhs', 'sub')
- grad_precond: float32 [3072, 9216], P('sub')
Inputs may be any that keep to these rules, and one draw needn't show every extreme that they name: `counts`: at least one subdomain has 48 live block rows. `send_rows`: for subdomain s, entries 0 to 5 are distinct live rows below counts[s] // 2 in increasing order, the first of them 0; entries 6 to 11 are distinct live rows from counts[s] // 2 on in increasing order, the last of them counts[s] - 1. Interface row j of the first group of subdomain s is coupled with interface row j of the second group of subdomain s - 1. `col_index`: index 6 + n is block n of the subdomain; indices below 6 and from 54 on are the blocks received from the previous and the next subdomain. Slot 0 of row n is 6 + n. A slot other than slot 0 that names 6 + n holds a zero block; rows that are not live hold only slot 0's block. `stiffness`: the operator A is symmetric and positive definite.
All inputs are finite; a program needn't handle non-finite values.
Results may differ from a plain program's by a relative error of at most 0.0003.
Values sent between devices are 32-bit elements; how exact they have to be, the bound alone decides.
A program may use at most 128 MiB of HBM per device.

v0:
```python
import jax
import jax.numpy as jnp
from jax import lax
from jax.sharding import PartitionSpec as P

BS = 96
K = 4
NBLK = 48
IF = 6
ITERS = 4


highest = lax.Precision.HIGHEST


def with_halo(array, sides, width):
    for axis, dim in sides:
        size, length = (lax.axis_size(axis), array.shape[dim])
        up = [(i, (i + 1) % size) for i in range(size - 1)]
        down = [(j, i) for i, j in up]
        last = lax.slice_in_dim(array, length - width, length, axis=dim)
        initial = lax.slice_in_dim(array, 0, width, axis=dim)
        before = lax.ppermute(last, axis, up)
        after = lax.ppermute(initial, axis, down)
        array = jnp.concatenate([before, array, after], axis=dim)
    return array


def local_dot(first_vec, second_vec):
    return jnp.sum(first_vec * second_vec, axis=(1, 2))


def widen(scalars):
    return scalars[:, None, None]


def precond_apply(weights, vector):
    projected = jnp.einsum("nab,rnb->rna", weights, vector, precision=highest)
    return (projected, vector + jnp.einsum("nab,rna->rnb", weights, projected, precision=highest))


def block_product(blocks, gathered):
    return jnp.einsum("nkab,rnkb->rna", blocks, gathered, precision=highest)


def stiff_apply(vector, blocks, columns, sending):
    outgoing = jnp.take(vector, sending, axis=1)
    framed = with_halo(outgoing, (("sub", 1),), IF)
    extended = jnp.concatenate([framed[:, :IF], vector, framed[:, 3 * IF :]], axis=1)
    return block_product(blocks, jnp.take(extended, columns, axis=1))


def norm_sum(first_vec, second_vec):
    return lax.psum(local_dot(first_vec, second_vec), "sub")


def grad_term(projected, zeta_bar, weight_zeta, resid_vec):
    first_part = jnp.einsum("rna,rnb->nab", projected, zeta_bar, precision=highest)
    return first_part + jnp.einsum("rna,rnb->nab", weight_zeta, resid_vec, precision=highest)


def shards(stiffness, precond, rhs_vec, cotangent, col_index, send_rows, counts):
    rhs_all, cot_all = (rhs_vec, cotangent)
    local_rhs = rhs_all.shape[0]
    blocks = stiffness.reshape(NBLK, K, BS, BS)
    weights = precond.reshape(NBLK, BS, BS)
    live_count = counts[0]
    sending = send_rows[0]
    live_mask = (jnp.arange(NBLK) < live_count).astype(jnp.float32)
    source = rhs_all.reshape(local_rhs, NBLK, BS) * live_mask[None, :, None]
    target = cot_all.reshape(local_rhs, NBLK, BS)
    residual = source
    first_proj, precon = precond_apply(weights, residual)
    first_res = residual
    direction = precon
    norm_now = norm_sum(residual, precon)
    solution = jnp.zeros_like(source)
    history = []
    for iteration in range(ITERS):
        applied = stiff_apply(direction, blocks, col_index, sending)
        curvature = lax.psum(local_dot(direction, applied), "sub")
        step_len = norm_now / curvature
        solution = solution + widen(step_len) * direction
        residual = residual - widen(step_len) * applied
        record = [direction, applied, step_len, curvature, norm_now]
        if iteration + 1 < ITERS:
            projected, precon = precond_apply(weights, residual)
            norm_next = norm_sum(residual, precon)
            ratio = norm_next / norm_now
            record = record + [residual, precon, projected, norm_next, ratio]
            direction = precon + widen(ratio) * direction
            norm_now = norm_next
        history.append(record)
    dir_bar = jnp.zeros_like(source)
    res_bar = jnp.zeros_like(source)
    norm_bar = jnp.zeros((local_rhs,), jnp.float32)
    grad_sum = jnp.zeros((NBLK, BS, BS), jnp.float32)
    for iteration in reversed(range(ITERS)):
        direction, applied, step_len, curvature, norm_now = history[iteration][:5]
        if iteration + 1 < ITERS:
            resid_next, precon, projected, norm_next, ratio = history[iteration][5:]
            ratio_bar, cot_dir = lax.psum(
                (local_dot(dir_bar, direction), local_dot(target, direction)), "sub"
            )
            norm_full = norm_bar + ratio_bar / norm_now
            zeta_bar = dir_bar + widen(norm_full) * resid_next
            weight_zeta, mapped = precond_apply(weights, zeta_bar)
            res_bar = res_bar + widen(norm_full) * precon + mapped
            res_image = lax.psum(local_dot(res_bar, applied), "sub")
            grad_sum = grad_sum + grad_term(projected, zeta_bar, weight_zeta, resid_next)
            dir_new = widen(ratio) * dir_bar
            norm_new = -ratio_bar * norm_next / (norm_now * norm_now)
        else:
            cot_dir = lax.psum(local_dot(target, direction), "sub")
            res_image = jnp.zeros_like(cot_dir)
            dir_new = jnp.zeros_like(source)
            norm_new = jnp.zeros_like(cot_dir)
        step_bar = cot_dir - res_image
        curv_bar = -step_bar * step_len / curvature
        dir_new = dir_new + widen(step_len) * target + widen(curv_bar) * applied
        image_bar = widen(curv_bar) * direction - widen(step_len) * res_bar
        dir_bar = dir_new + stiff_apply(image_bar, blocks, col_index, sending)
        norm_bar = norm_new + step_bar / curvature
    zeta_bar = dir_bar + widen(norm_bar) * first_res
    weight_zeta = jnp.einsum("nab,rnb->rna", weights, zeta_bar, precision=highest)
    grad_sum = grad_sum + grad_term(first_proj, zeta_bar, weight_zeta, first_res)
    grad_sum = lax.psum(grad_sum, "rhs")
    flat_solution = solution.reshape(local_rhs, NBLK * BS)
    return (flat_solution, grad_sum.reshape(NBLK, BS * BS))


def solution(mesh):
    in_specs = (
        P("sub", None, None),
        P("sub", None),
        P("rhs", "sub"),
        P("rhs", "sub"),
        P("sub", None),
        P("sub", None),
        P("sub"),
    )
    out_specs = (P("rhs", "sub"), P("sub", None))
    return jax.shard_map(shards, mesh=mesh, in_specs=in_specs, out_specs=out_specs, check_vma=False)
```

profile of v0, /device:TPU:1, one launch (start us, length us, event | category | flops | bytes accessed | tf_op | source)
XLA Modules:
  0.0 1994.4 jit_solution(11728397006781931206)
XLA Ops:
  12.3 3.8 convolution_bitcast_fusion.22
  18.9 4.6 collective-permute-start
  25.8 10.6 reshape.54
  37.3 10.5 multiply_reduce_fusion.16
  47.8 127.8 %all-reduce.4 = (f32[2]{0:T(128)S(1)}, f32[2]{0:T(128)S(1)}) all-reduce(f32[2]{0:T(128)S(1)} %get-tuple-element.10, f32[2]{0:T(128)S(1)} %get-tuple-element.9), channel_id=1, replica_groups=mesh['sub'=64,'rhs'=4] {'sub'}, use_global_device_ids=true, to_apply=%region_1.0 | all-reduce | flops 4 | bytes 32 | tf_op jit(solution)/shard_map/psum | solution.py:54
  175.8 3.8 convolution_bitcast_fusion.20
  181.7 127.4 %psum.135 = f32[2]{0:T(128)S(1)} all-reduce(f32[2]{0:T(128)S(1)} %get-tuple-element.44), channel_id=1, replica_groups=mesh['sub'=64,'rhs'=4] {'sub'}, use_global_device_ids=true, to_apply=%region_5.8 | all-reduce | flops 2 | bytes 16 | tf_op jit(solution)/shard_map/psum | solution.py:54
  314.3 2.5 collective-permute-done.3
  317.7 10.5 multiply_reduce_fusion.14
  328.2 122.2 %psum.136 = f32[2]{0:T(128)S(1)} all-reduce(f32[2]{0:T(128)S(1)} %get-tuple-element.46), channel_id=1, replica_groups=mesh['sub'=64,'rhs'=4] {'sub'}, use_global_device_ids=true, to_apply=%region_7.10 | all-reduce | flops 2 | bytes 16 | tf_op jit(solution)/shard_map/psum | solution.py:81
  450.5 3.8 convolution_bitcast_fusion.18
  456.5 125.9 %psum.137 = f32[2]{0:T(128)S(1)} all-reduce(f32[2]{0:T(128)S(1)} %get-tuple-element.48), channel_id=1, replica_groups=mesh['sub'=64,'rhs'=4] {'sub'}, use_global_device_ids=true, to_apply=%region_9.12 | all-reduce | flops 2 | bytes 16 | tf_op jit(solution)/shard_map/psum | solution.py:54
  587.5 2.5 collective-permute-done.5
  591.0 10.5 multiply_reduce_fusion.12
  601.5 122.2 %psum.138 = f32[2]{0:T(128)S(1)} all-reduce(f32[2]{0:T(128)S(1)} %get-tuple-element.50), channel_id=1, replica_groups=mesh['sub'=64,'rhs'=4] {'sub'}, use_global_device_ids=true, to_apply=%region_11.14 | all-reduce | flops 2 | bytes 16 | tf_op jit(solution)/shard_map/psum | solution.py:81
  723.8 3.8 convolution_bitcast_fusion.16
  729.8 125.9 %psum.139 = f32[2]{0:T(128)S(1)} all-reduce(f32[2]{0:T(128)S(1)} %get-tuple-element.52), channel_id=1, replica_groups=mesh['sub'=64,'rhs'=4] {'sub'}, use_global_device_ids=true, to_apply=%region_13.16 | all-reduce | flops 2 | bytes 16 | tf_op jit(solution)/shard_map/psum | solution.py:54
  864.3 11.1 multiply_reduce_fusion.1
  875.5 122.0 %all-reduce.3 = (f32[2]{0:T(128)S(1)}, f32[2]{0:T(128)S(1)}) all-reduce(f32[2]{0:T(128)S(1)} %get-tuple-element.6, f32[2]{0:T(128)S(1)} %get-tuple-element.5), channel_id=1, replica_groups=mesh['sub'=64,'rhs'=4] {'sub'}, use_global_device_ids=true, to_apply=%region_15.18 | all-reduce | flops 4 | bytes 32 | tf_op jit(solution)/shard_map/psum | solution.py:81
  1000.7 4.2 collective-permute-start.9
  1006.6 10.5 multiply_reduce_fusion.8
  1017.1 123.4 %psum.142 = f32[2]{0:T(128)S(1)} all-reduce(f32[2]{0:T(128)S(1)} %get-tuple-element.55), channel_id=1, replica_groups=mesh['sub'=64,'rhs'=4] {'sub'}, use_global_device_ids=true, to_apply=%region_19.22 | all-reduce | flops 2 | bytes 16 | tf_op jit(solution)/shard_map/psum | solution.py:102
  1140.6 3.8 convolution_bitcast_fusion.14
  1146.6 5.2 fusion.64
  1151.9 124.5 %all-reduce.2 = (f32[2]{0:T(128)S(1)}, f32[2]{0:T(128)S(1)}) all-reduce(f32[2]{0:T(128)S(1)} %copy-done.43, f32[2]{0:T(128)S(1)} %get-tuple-element.57), channel_id=1, replica_groups=mesh['sub'=64,'rhs'=4] {'sub'}, use_global_device_ids=true, to_apply=%region_21.24 | all-reduce | flops 4 | bytes 32 | tf_op jit(solution)/shard_map/psum | solution.py:102
  1279.7 2.6 collective-permute-start.11
  1282.2 5.4 fusion.63
  1288.6 10.5 multiply_reduce_fusion.5
  1299.1 123.0 %psum.145 = f32[2]{0:T(128)S(1)} all-reduce(f32[2]{0:T(128)S(1)} %get-tuple-element.59), channel_id=1, replica_groups=mesh['sub'=64,'rhs'=4] {'sub'}, use_global_device_ids=true, to_apply=%region_25.28 | all-reduce | flops 2 | bytes 16 | tf_op jit(solution)/shard_map/psum | solution.py:102
  1422.2 3.8 convolution_bitcast_fusion.12
  1428.2 5.2 fusion.66
  1433.5 125.2 %all-reduce.1 = (f32[2]{0:T(128)S(1)}, f32[2]{0:T(128)S(1)}) all-reduce(f32[2]{0:T(128)S(1)} %copy-done.42, f32[2]{0:T(128)S(1)} %get-tuple-element.61), channel_id=1, replica_groups=mesh['sub'=64,'rhs'=4] {'sub'}, use_global_device_ids=true, to_apply=%region_27.30 | all-reduce | flops 4 | bytes 32 | tf_op jit(solution)/shard_map/psum | solution.py:102
  1561.3 2.7 collective-permute-start.13
  1564.0 5.3 fusion.65
  1570.2 10.5 multiply_reduce_fusion.2
  1580.7 123.3 %psum.148 = f32[2]{0:T(128)S(1)} all-reduce(f32[2]{0:T(128)S(1)} %get-tuple-element.63), channel_id=1, replica_groups=mesh['sub'=64,'rhs'=4] {'sub'}, use_global_device_ids=true, to_apply=%region_31.34 | all-reduce | flops 2 | bytes 16 | tf_op jit(solution)/shard_map/psum | solution.py:102
  1704.1 3.8 convolution_bitcast_fusion.10
  1710.1 5.2 fusion.68
  1715.4 125.2 %all-reduce = (f32[2]{0:T(128)S(1)}, f32[2]{0:T(128)S(1)}) all-reduce(f32[2]{0:T(128)S(1)} %copy-done.41, f32[2]{0:T(128)S(1)} %get-tuple-element.65), channel_id=1, replica_groups=mesh['sub'=64,'rhs'=4] {'sub'}, use_global_device_ids=true, to_apply=%region_33.36 | all-reduce | flops 4 | bytes 32 | tf_op jit(solution)/shard_map/psum | solution.py:102
  1843.3 2.6 collective-permute-start.15
  1845.9 5.3 fusion.67
  1852.1 10.8 fusion.1
  1862.9 3.8 convolution_bitcast_fusion.8
  1866.7 3.9 fusion.69
  1870.6 4.3 add_add_fusion
  1874.9 2.5 reshape.57
  1878.2 106.4 %all-reduce.7.cloned.1.call-done = f32[48,9216]{1,0:T(8,128)} async-done(((f32[48,9216]{1,0:T(8,128)}), f32[48,9216]{1,0:T(8,128)}) %all-reduce.7.cloned.1.call-update) | async-done | bytes 1769488 | tf_op jit(solution)/shard_map/psum | solution.py:127
  1984.6 2.8 copy.72
  (208 shorter events, 61.8 us)
Async XLA Ops:
  7.2 1977.4 %all-reduce.7.cloned.1.call-start = ((), (), s32[]{:S(2)}) async-start(), calls=%async_computation | async-start | bytes 3538944 | tf_op jit(solution)/shard_map/psum | solution.py:127
  12.3 13.1 copy-start.13
  18.9 17.5 collective-permute-start
  23.5 12.9 collective-permute-start.1
  175.6 133.5 %copy-start.19 = (f32[2]{0:T(128)}, f32[2]{0:T(128)S(1)}, u32[]{:S(2)}) copy-start(f32[2]{0:T(128)S(1)} %get-tuple-element.19) | copy-start | bytes 28
  179.5 148.7 %copy-start.6 = (f32[2,48,96]{2,0,1:T(2,128)}, f32[2,48,96]{2,0,1:T(2,128)S(1)}, u32[]{:S(2)}) copy-start(f32[2,48,96]{2,0,1:T(2,128)S(1)} %convolution_bitcast_fusion.20) | copy-start | bytes 110596
  309.9 4.3 collective-permute-start.2
  311.8 4.9 collective-permute-start.3
  454.2 128.2 %copy-start.8 = (f32[2,48,96]{2,0,1:T(2,128)}, f32[2,48,96]{2,0,1:T(2,128)S(1)}, u32[]{:S(2)}) copy-start(f32[2,48,96]{2,0,1:T(2,128)S(1)} %convolution_bitcast_fusion.18) | copy-start | bytes 110596
  582.4 19.0 copy-start.16
  583.2 4.3 collective-permute-start.4
  585.1 4.9 collective-permute-start.5
  723.8 137.1 %copy-start.12 = (f32[2,4608]{1,0:T(2,128)S(1)}, f32[2,4608]{1,0:T(2,128)}, u32[]{:S(2)}) copy-start(f32[2,4608]{1,0:T(2,128)} %param.14) | copy-start | bytes 110596
  727.6 130.9 %copy-start.10 = (f32[2,48,96]{2,0,1:T(2,128)}, f32[2,48,96]{2,0,1:T(2,128)S(1)}, u32[]{:S(2)}) copy-start(f32[2,48,96]{2,0,1:T(2,128)S(1)} %convolution_bitcast_fusion.16) | copy-start | bytes 110596
  855.8 141.7 %copy-start.27 = (f32[2]{0:T(128)}, f32[2]{0:T(128)S(1)}, u32[]{:S(2)}) copy-start(f32[2]{0:T(128)S(1)} %psum.139) | copy-start | bytes 28
  855.8 19.7 copy-start.18
  856.5 4.5 collective-permute-start.6
  858.5 4.9 collective-permute-start.7
  998.8 6.2 collective-permute-start.8
  1000.7 4.9 collective-permute-start.9
  1006.6 134.0 %copy-start.38 = (f32[2]{0:T(128)S(1)}, f32[2]{0:T(128)}, u32[]{:S(2)}) copy-start(f32[2]{0:T(128)} %copy-done.37) | copy-start | bytes 28
  1006.6 133.9 %copy-start.40 = (f32[2]{0:T(128)S(1)}, f32[2]{0:T(128)}, u32[]{:S(2)}) copy-start(f32[2]{0:T(128)} %copy-done.39) | copy-start | bytes 28
  1144.4 132.0 %copy-start.25 = (f32[2]{0:T(128)S(1)}, f32[2]{0:T(128)}, u32[]{:S(2)}) copy-start(f32[2]{0:T(128)} %copy-done.24) | copy-start | bytes 28
  1144.4 137.8 %copy-start.11 = (f32[2,48,96]{2,0,1:T(2,128)S(1)}, f32[2,48,96]{2,0,1:T(2,128)}, u32[]{:S(2)}) copy-start(f32[2,48,96]{2,0,1:T(2,128)} %copy-done.10) | copy-start | bytes 110596
  1277.7 9.9 collective-permute-start.10
  1279.7 8.0 collective-permute-start.11
  1288.5 133.6 %copy-start.26 = (f32[2]{0:T(128)S(1)}, f32[2]{0:T(128)}, u32[]{:S(2)}) copy-start(f32[2]{0:T(128)} %copy-done.24) | copy-start | bytes 28
  1288.5 133.6 %copy-start.28 = (f32[2]{0:T(128)S(1)}, f32[2]{0:T(128)}, u32[]{:S(2)}) copy-start(f32[2]{0:T(128)} %copy-done.27) | copy-start | bytes 28
  1288.5 133.5 %copy-start.32 = (f32[2]{0:T(128)S(1)}, f32[2]{0:T(128)}, u32[]{:S(2)}) copy-start(f32[2]{0:T(128)} %copy-done.31) | copy-start | bytes 28
  1288.5 133.5 %copy-start.34 = (f32[2]{0:T(128)S(1)}, f32[2]{0:T(128)}, u32[]{:S(2)}) copy-start(f32[2]{0:T(128)} %copy-done.33) | copy-start | bytes 28
  1288.5 133.5 %copy-start.36 = (f32[2]{0:T(128)S(1)}, f32[2]{0:T(128)}, u32[]{:S(2)}) copy-start(f32[2]{0:T(128)} %copy-done.35) | copy-start | bytes 28
  1426.0 132.6 %copy-start.22 = (f32[2]{0:T(128)S(1)}, f32[2]{0:T(128)}, u32[]{:S(2)}) copy-start(f32[2]{0:T(128)} %copy-done.21) | copy-start | bytes 28
  1426.0 138.0 %copy-start.9 = (f32[2,48,96]{2,0,1:T(2,128)S(1)}, f32[2,48,96]{2,0,1:T(2,128)}, u32[]{:S(2)}) copy-start(f32[2,48,96]{2,0,1:T(2,128)} %copy-done.8) | copy-start | bytes 110596
  1428.2 142.0 %copy-start.17 = (f32[2]{0:T(128)S(1)}, f32[2]{0:T(128)}, u32[]{:S(2)}) copy-start(f32[2]{0:T(128)} %copy-done.16) | copy-start | bytes 28
  1559.4 9.9 collective-permute-start.12
  1561.3 8.0 collective-permute-start.13
  1570.2 133.8 %copy-start.20 = (f32[2]{0:T(128)S(1)}, f32[2]{0:T(128)}, u32[]{:S(2)}) copy-start(f32[2]{0:T(128)} %copy-done.19) | copy-start | bytes 28
  1570.2 133.8 %copy-start.23 = (f32[2]{0:T(128)S(1)}, f32[2]{0:T(128)}, u32[]{:S(2)}) copy-start(f32[2]{0:T(128)} %copy-done.21) | copy-start | bytes 28
  1570.2 133.8 %copy-start.30 = (f32[2]{0:T(128)S(1)}, f32[2]{0:T(128)}, u32[]{:S(2)}) copy-start(f32[2]{0:T(128)} %copy-done.29) | copy-start | bytes 28
  1707.9 132.6 %copy-start.45 = (f32[2]{0:T(128)S(1)}, f32[2]{0:T(128)}, u32[]{:S(2)}) copy-start(f32[2]{0:T(128)} %copy-done.44) | copy-start | bytes 28
  1707.9 138.0 %copy-start.7 = (f32[2,48,96]{2,0,1:T(2,128)S(1)}, f32[2,48,96]{2,0,1:T(2,128)}, u32[]{:S(2)}) copy-start(f32[2,48,96]{2,0,1:T(2,128)} %copy-done.6) | copy-start | bytes 110596
  1710.1 142.0 %copy-start.15 = (f32[2]{0:T(128)S(1)}, f32[2]{0:T(128)}, u32[]{:S(2)}) copy-start(f32[2]{0:T(128)} %copy-done.14) | copy-start | bytes 28
  1841.3 9.8 collective-permute-start.14
  1843.3 7.9 collective-permute-start.15
  1852.1 18.4 copy-start.2
  1852.1 18.4 copy-start.3
  1852.1 18.4 copy-start.4
  1852.1 18.4 copy-start.5
  (15 other events, 68.9 us)
Sparse Core Ops, SparseCore 0:
  1877.6 106.9 all-reduce.6
where the time goes:
time: 2000 us; the launch traced here: 1990 us
  blocking collectives  1620 us (81%)
  matrix products  170 us (8%)
  waiting for transfers between devices  115 us (6%)
  starting transfers between devices  39.2 us (2%)
  local copies, waits for them, and re-layouts  32.9 us (2%)
    psum x6, blocking collectives, shards(): lax.psum((local_dot(dir_bar, direction), local_dot(target, direction)), '...  745 us
    psum x4, blocking collectives, norm_sum(): return lax.psum(local_dot(first_vec, second_vec), 'sub')  507 us
    psum x3, blocking collectives, shards(): curvature = lax.psum(local_dot(direction, applied), 'sub')  366 us
    psum x1, waiting for transfers between devices, shards(): grad_sum = lax.psum(grad_sum, 'rhs')  106 us
    dot_general x8, matrix products, block_product(): return jnp.einsum('nkab,rnkb->rna', blocks, gathered, precision=highest)  84.9 us
  transfers between devices with their start and end apart: 17, of which 5 were waited for; matrix products, arithmetic and copies ran while one was open for 1% of the time, Pallas kernels for 0%

commit v1 on v0

v1 whole, which is shorter than its diff:
```python
import functools

import jax
import jax.numpy as jnp
from jax import lax
from jax.experimental import pallas as pl
from jax.experimental.pallas import tpu as pltpu
from jax.sharding import PartitionSpec as P

BS = 96
K = 4
NBLK = 48
IF = 6
ITERS = 4
LR = 2
LANES = 128
TILES = NBLK // 8
CHUNKS = BS * BS // LANES
GROUPS = CHUNKS // 3
VEC = LR * NBLK
ROWS = LR * BS * NBLK // LANES
PLANE = 8
UNROLL = 6
HALOS = 8
REDS = 6
EXT = 64
MESH = pl.DeviceIdType.MESH


def lane_iota():
    return lax.broadcasted_iota(jnp.int32, (8, LANES), 1)


def patterns(x, lane):
    far = pltpu.roll(x, 96, 1)
    mid = pltpu.roll(x, 64, 1)
    near = pltpu.roll(x, 32, 1)
    return (
        jnp.where(lane < 96, x, far),
        jnp.where(lane < 64, far, mid),
        jnp.where(lane < 32, mid, near),
    )


def row_parts(p, lane):
    zero = jnp.zeros_like(p[0])
    return (
        jnp.where(lane < 96, p[0], zero),
        jnp.where(lane < 64, p[1], jnp.where(lane >= 96, p[0], zero)),
        jnp.where(lane >= 64, p[1], jnp.where(lane < 32, p[2], zero)),
        jnp.where(lane >= 32, p[2], zero),
    )


def rows_to_chunks(r, lane):
    far = pltpu.roll(r[1], 96, 1)
    mid = pltpu.roll(r[2], 64, 1)
    return (
        jnp.where(lane < 96, r[0], far),
        jnp.where(lane < 64, far, mid),
        jnp.where(lane < 32, mid, pltpu.roll(r[3], 32, 1)),
    )


def chunks_to_rows(c, lane):
    zero = jnp.zeros_like(c[0])
    rows = (
        c[0],
        pltpu.roll(jnp.where(lane >= 96, c[0], c[1]), 32, 1),
        pltpu.roll(jnp.where(lane >= 64, c[1], c[2]), 64, 1),
        pltpu.roll(c[2], 96, 1),
    )
    return [jnp.where(lane < 96, r, zero) for r in rows]


def kernel(
    planes, nrhs,
    col_ref, send_ref, count_ref, rhs_ref, cot_ref, stiff_hbm, pre_hbm,
    sol_ref, grad_hbm,
    raw, blocks, weights, colx, ext, gat, nvec, hvec, tvec, tmv, utv, atv, yv, kv, xv,
    pbv, rbv, arbv,
    ph, qh, sh, zh, wh, rh, uh, scr, hsend, hrecv, rb1, rb2, fl, fr, gb, go,
    load_sem, out_sem, hs_sem, hr_sem, r1s, r1r, r2s, r2r, fs_sem, fr_sem,
):
    sub = lax.axis_index("sub")
    me = lax.axis_index("rhs")
    nsub = planes * PLANE
    plane = lax.div(sub, PLANE)
    spot = lax.rem(sub, PLANE)
    lane = lane_iota()

    def in_plane(d):
        return plane * PLANE + lax.rem(spot + d, PLANE)

    def across(d):
        return lax.rem(plane + d, planes) * PLANE + spot

    pre_copy = pltpu.make_async_copy(pre_hbm, weights, load_sem.at[TILES])
    pre_copy.start()
    stiff_copies = [
        pltpu.make_async_copy(stiff_hbm.at[t], raw.at[t], load_sem.at[t])
        for t in range(TILES)
    ]
    for copy in stiff_copies:
        copy.start()

    barrier = pltpu.get_barrier_semaphore()
    peers = 0
    for d in range(1, PLANE):
        pl.semaphore_signal(barrier, inc=1, device_id={"sub": in_plane(d)}, device_id_type=MESH)
        peers += 1
    for d in range(1, planes):
        pl.semaphore_signal(barrier, inc=1, device_id={"sub": across(d)}, device_id_type=MESH)
        peers += 1
    for d in range(1, nrhs):
        pl.semaphore_signal(barrier, inc=1, device_id={"rhs": lax.rem(me + d, nrhs)}, device_id_type=MESH)
        peers += 1
    before = lax.rem(sub + nsub - 1, nsub)
    after = lax.rem(sub + 1, nsub)
    for other in (before, after):
        pl.semaphore_signal(barrier, inc=1, device_id={"sub": other}, device_id_type=MESH)
        peers += 1

    for n in range(NBLK):
        for k in range(1, K):
            c = col_ref[n, k]
            colx[n * K + k] = jnp.where(
                c < IF, c + NBLK, jnp.where(c < IF + NBLK, c - IF, c + 8 - IF)
            )
    hsend[...] = jnp.zeros_like(hsend)
    for ref in (ph, qh, sh):
        ref[pl.ds(0, VEC), :] = jnp.zeros((VEC, LANES), jnp.float32)
    for ref in (yv, kv, xv, rbv, arbv):
        ref[...] = jnp.zeros_like(ref)

    lane12 = lax.broadcasted_iota(jnp.int32, (12, LANES), 1)
    row12 = lax.broadcasted_iota(jnp.int32, (12, LANES), 0)
    live = count_ref[0]
    for r in range(LR):
        chunks = [rhs_ref[pl.ds(2 * i + r, 12, stride=6), :] for i in range(3)]
        for j, row in enumerate(chunks_to_rows(chunks, lane12)):
            row = jnp.where(row12 * 4 + j < live, row, jnp.zeros_like(row))
            rh[pl.ds(r * NBLK + j, 12, stride=4), :] = row
        chunks = [cot_ref[pl.ds(2 * i + r, 12, stride=6), :] for i in range(3)]
        for j, row in enumerate(chunks_to_rows(chunks, lane12)):
            tvec[pl.ds(r * NBLK + j, 12, stride=4), :] = row

    def precondition(src, base, dst, dst_base, slot):
        full = slot is not None

        def tile(t, _):
            x = [src[pl.ds(pl.multiple_of(base + r * NBLK + 8 * t, 8), 8), :] for r in range(LR)]
            pat = [patterns(v, lane) for v in x]
            zero = jnp.zeros((8, LANES), jnp.float32)

            def step(s, carry):
                proj, acc = carry
                proj, acc = list(proj), [list(a) for a in acc]
                for q in range(UNROLL):
                    g = s * UNROLL + q
                    w = [weights[t, 3 * g + i] for i in range(3)]
                    for r in range(LR):
                        parts = row_parts([w[i] * pat[r][i] for i in range(3)], lane)
                        sums = [
                            jnp.broadcast_to(jnp.sum(p, axis=1, keepdims=True), (8, LANES))
                            for p in parts
                        ]
                        for j in range(4):
                            proj[r] = jnp.where(lane == 4 * g + j, sums[j], proj[r])
                        if full:
                            acc[r][0] += w[0] * jnp.where(lane < 96, sums[0], sums[1])
                            acc[r][1] += w[1] * jnp.where(lane < 64, sums[1], sums[2])
                            acc[r][2] += w[2] * jnp.where(lane < 32, sums[2], sums[3])
                return tuple(proj), tuple(tuple(a) for a in acc)

            start = ((zero,) * LR, ((zero,) * 3,) * LR)
            proj, acc = lax.fori_loop(0, GROUPS // UNROLL, step, start)
            for r in range(LR):
                dst[pl.ds(pl.multiple_of(dst_base + r * NBLK + 8 * t, 8), 8), :] = proj[r]
                if full:
                    a = acc[r]
                    total = (
                        a[0]
                        + pltpu.roll(jnp.where(lane >= 96, a[0], a[1]), 32, 1)
                        + pltpu.roll(jnp.where(lane >= 64, a[1], a[2]), 64, 1)
                        + pltpu.roll(a[2], 96, 1)
                    )
                    ext[slot, pl.ds(pl.multiple_of(r * EXT + 8 * t, 8), 8), :] = x[r] + jnp.where(
                        lane < 96, total, zero
                    )
            return 0

        lax.fori_loop(0, TILES, tile, 0)

    def halo_copies(h):
        return (
            pltpu.make_async_remote_copy(
                src_ref=hsend.at[h, 0], dst_ref=hrecv.at[h, 1],
                send_sem=hs_sem.at[h, 0], recv_sem=hr_sem.at[h, 1],
                device_id={"sub": before}, device_id_type=MESH,
            ),
            pltpu.make_async_remote_copy(
                src_ref=hsend.at[h, 1], dst_ref=hrecv.at[h, 0],
                send_sem=hs_sem.at[h, 1], recv_sem=hr_sem.at[h, 0],
                device_id={"sub": after}, device_id_type=MESH,
            ),
        )

    def halo_start(h, slot):
        for side in range(2):
            for j in range(IF):
                idx = send_ref[0, side * IF + j]
                for r in range(LR):
                    hsend[h, side, pl.ds(r * 8 + j, 1), :] = ext[slot, pl.ds(r * EXT + idx, 1), :]
        for copy in halo_copies(h):
            copy.start()

    def halo_finish(h, slot):
        for copy in halo_copies(h):
            copy.wait_recv()
        for side in range(2):
            edge = jnp.where(sub == (0 if side == 0 else nsub - 1), 0, 1)
            inside = jnp.broadcast_to(edge, (8, LANES)) > 0
            for r in range(LR):
                v = hrecv[h, side, pl.ds(r * 8, 8), :]
                ext[slot, pl.ds(r * EXT + NBLK + 8 * side, 8), :] = jnp.where(
                    inside, v, jnp.zeros_like(v)
                )

    def halo_sent(h):
        for copy in halo_copies(h):
            copy.wait_send()

    def stiffness(slot, dst):
        def gather(s, _):
            for q in range(4):
                n = s * 4 + q
                for k in range(1, K):
                    c = colx[n * K + k]
                    for r in range(LR):
                        gat[pl.ds(((k - 1) * LR + r) * NBLK + n, 1), :] = ext[
                            slot, pl.ds(r * EXT + c, 1), :
                        ]
            return 0

        lax.fori_loop(0, NBLK // 4, gather, 0)

        def tile(t, _):
            pat = []
            for r in range(LR):
                own = ext[slot, pl.ds(pl.multiple_of(r * EXT + 8 * t, 8), 8), :]
                rest = [
                    gat[pl.ds(pl.multiple_of(((k - 1) * LR + r) * NBLK + 8 * t, 8), 8), :]
                    for k in range(1, K)
                ]
                pat.append([patterns(v, lane) for v in [own] + rest])
            zero = jnp.zeros((8, LANES), jnp.float32)

            def step(s, out):
                out = list(out)
                for q in range(UNROLL):
                    g = s * UNROLL + q
                    prod = [[None] * 3 for _ in range(LR)]
                    for i in range(3):
                        a = [blocks[t, 3 * g + i, k] for k in range(K)]
                        for r in range(LR):
                            prod[r][i] = (a[0] * pat[r][0][i] + a[1] * pat[r][1][i]) + (
                                a[2] * pat[r][2][i] + a[3] * pat[r][3][i]
                            )
                    for r in range(LR):
                        for j, p in enumerate(row_parts(prod[r], lane)):
                            s_j = jnp.broadcast_to(jnp.sum(p, axis=1, keepdims=True), (8, LANES))
                            out[r] = jnp.where(lane == 4 * g + j, s_j, out[r])
                return tuple(out)

            out = lax.fori_loop(0, GROUPS // UNROLL, step, (zero,) * LR)
            for r in range(LR):
                dst[pl.ds(pl.multiple_of(r * NBLK + 8 * t, 8), 8), :] = out[r]
            return 0

        lax.fori_loop(0, TILES, tile, 0)

    def stage_copy(buf, ssem, rsem, rd, d, mine, target):
        at = rd * 8 + mine
        return pltpu.make_async_remote_copy(
            src_ref=buf.at[at], dst_ref=buf.at[at],
            send_sem=ssem.at[rd * 8 + d], recv_sem=rsem.at[at],
            device_id={"sub": target}, device_id_type=MESH,
        )

    def arrived(buf, ssem, rsem, rd, d, source, target):
        at = rd * 8 + source
        pltpu.make_async_remote_copy(
            src_ref=buf.at[at], dst_ref=buf.at[at],
            send_sem=ssem.at[rd * 8 + d], recv_sem=rsem.at[at],
            device_id={"sub": target}, device_id_type=MESH,
        ).wait_recv()

    def sum_start(rd, pairs):
        tiles = []
        srow = lax.broadcasted_iota(jnp.int32, (8, LANES), 0)
        for r in range(LR):
            tile = jnp.zeros((8, LANES), jnp.float32)
            for d, (a, b) in enumerate(pairs):
                row = jnp.sum(a[r] * b[r], axis=0, keepdims=True)
                tile = jnp.where(srow == d, jnp.broadcast_to(row, (8, LANES)), tile)
            tiles.append(jnp.sum(tile, axis=1, keepdims=True))
        rb1[rd * 8 + spot] = jnp.where(
            lane < 64,
            jnp.broadcast_to(tiles[0], (8, LANES)),
            jnp.broadcast_to(tiles[1], (8, LANES)),
        )
        for d in range(1, PLANE):
            stage_copy(rb1, r1s, r1r, rd, d, spot, in_plane(d)).start()

    def sum_middle(rd):
        for d in range(1, PLANE):
            arrived(rb1, r1s, r1r, rd, d, lax.rem(spot + d, PLANE), in_plane(d))
        v = [rb1[rd * 8 + s] for s in range(PLANE)]
        rb2[rd * 8 + plane] = ((v[0] + v[1]) + (v[2] + v[3])) + ((v[4] + v[5]) + (v[6] + v[7]))
        for d in range(1, planes):
            stage_copy(rb2, r2s, r2r, rd, d, plane, across(d)).start()

    def sum_finish(rd):
        for d in range(1, planes):
            arrived(rb2, r2s, r2r, rd, d, lax.rem(plane + d, planes), across(d))
        v = rb2[rd * 8]
        for s in range(1, planes):
            v = v + rb2[rd * 8 + s]
        swapped = pltpu.roll(v, 64, 1)
        for d in range(1, PLANE):
            stage_copy(rb1, r1s, r1r, rd, d, spot, in_plane(d)).wait_send()
        for d in range(1, planes):
            stage_copy(rb2, r2s, r2r, rd, d, plane, across(d)).wait_send()
        return (jnp.where(lane < 64, v, swapped), jnp.where(lane < 64, swapped, v))

    def factor_row(src, j, kind):
        return pl.multiple_of(((src * ITERS + j) * 2 + kind) * VEC, 8)

    def factor_copy(buf, left, j, kind, d, src, target):
        at = factor_row(src, j, kind)
        piece = (j * 2 + left) * 2 + kind
        return pltpu.make_async_remote_copy(
            src_ref=buf.at[pl.ds(at, VEC), :], dst_ref=buf.at[pl.ds(at, VEC), :],
            send_sem=fs_sem.at[piece * 4 + d], recv_sem=fr_sem.at[piece * 4 + src],
            device_id={"rhs": target}, device_id_type=MESH,
        )

    def factor_send(buf, left, j, kind):
        for d in range(1, nrhs):
            factor_copy(buf, left, j, kind, d, me, lax.rem(me + d, nrhs)).start()

    def rows(ref, i):
        return [
            ref[pl.ds(pl.multiple_of(i * VEC + r * NBLK, 8), NBLK), :] for r in range(LR)
        ]

    def put(ref, i, v):
        for r in range(LR):
            ref[pl.ds(pl.multiple_of(i * VEC + r * NBLK, 8), NBLK), :] = v[r]

    def put_at(ref, base, v):
        for r in range(LR):
            ref[pl.ds(pl.multiple_of(base + r * NBLK, 8), NBLK), :] = v[r]

    def ext_rows(slot):
        return [ext[slot, pl.ds(r * EXT, NBLK), :] for r in range(LR)]

    def axpy(x, s, y):
        return [a + c * b for a, c, b in zip(x, s, y)]

    def scale(s, y):
        return [c * b for c, b in zip(s, y)]

    def keep(kind, i, v):
        for r in range(LR):
            scr[pl.ds((r * 6 + kind) * ITERS + i, 1), :] = v[r]

    def kept(kind, i):
        return [scr[pl.ds((r * 6 + kind) * ITERS + i, 1), :] for r in range(LR)]

    pre_copy.wait()
    precondition(rh, 0, uh, 0, 0)
    pl.semaphore_wait(barrier, peers)
    halo_start(0, 0)
    put(zh, 0, ext_rows(0))
    precondition(tvec, 0, utv, 0, 1)
    halo_start(1, 1)
    put(tmv, 0, ext_rows(1))
    for t in range(TILES):
        stiff_copies[t].wait()

        def relay(s, _, t=t):
            for q in range(4):
                c = s * 4 + q
                for k in range(K):
                    blocks[t, c, k] = raw[t, pl.ds(c * K + k, 8, stride=CHUNKS * K), :]
            return 0

        lax.fori_loop(0, CHUNKS // 4, relay, 0)
    halo_finish(0, 0)
    stiffness(0, nvec)
    put(wh, 0, rows(nvec, 0))
    halo_finish(1, 1)
    stiffness(1, atv)
    halo_sent(0)
    halo_sent(1)

    def forward(i, carry):
        rho_old, gamma_old, c_old = carry[:3]
        z, w, res, t = rows(zh, i), rows(wh, i), rows(rh, i), rows(tvec, 0)
        q_old, s_old = rows(qh, i), rows(sh, i)
        sum_start(
            i,
            (
                (res, z), (z, w), (z, q_old), (t, z),
                (t, s_old), (w, s_old), (q_old, s_old),
            ),
        )
        precondition(wh, i * VEC, hvec, 0, 0)
        halo_start(2 + i, 0)
        at = factor_row(me, i, 0)
        put_at(fl, at, rows(uh, i))
        at = factor_row(me, i, 1)
        put_at(fr, at, rows(rh, i))
        factor_send(fl, 1, i, 0)
        factor_send(fr, 0, i, 1)
        sum_middle(i)
        halo_finish(2 + i, 0)
        stiffness(0, nvec)
        halo_sent(2 + i)
        tot = sum_finish(i)
        val = [[tot[r][d : d + 1, :] for r in range(LR)] for d in range(7)]
        rho, za, zq, tz = val[:4]
        first = jnp.broadcast_to(jnp.where(i == 0, 1, 0), (1, LANES)) > 0
        beta = [jnp.where(first, 0.0, a / b) for a, b in zip(rho, rho_old)]
        gamma = [
            za[r] + beta[r] * (2.0 * zq[r] + beta[r] * gamma_old[r]) for r in range(LR)
        ]
        c = axpy(tz, beta, c_old)
        alpha = [a / b for a, b in zip(rho, gamma)]
        minus = [-a for a in alpha]
        for kind, v in enumerate((alpha, gamma, rho, beta, c, zq)):
            keep(kind, i, v)
        p = axpy(rows(zh, i), beta, rows(ph, i))
        put(ph, i + 1, p)
        put(xv, 0, axpy(rows(xv, 0), alpha, p))
        q = axpy(rows(wh, i), beta, rows(qh, i))
        put(qh, i + 1, q)
        put(rh, i + 1, axpy(rows(rh, i), minus, q))
        s = axpy(ext_rows(0), beta, rows(sh, i))
        put(sh, i + 1, s)
        put(zh, i + 1, axpy(rows(zh, i), minus, s))
        y = axpy(rows(nvec, 0), beta, rows(yv, 0))
        put(yv, 0, y)
        put(wh, i + 1, axpy(rows(wh, i), minus, y))
        k = axpy(rows(hvec, 0), beta, rows(kv, 0))
        put(kv, 0, k)
        put(uh, i + 1, axpy(rows(uh, i), minus, k))
        return (
            tuple(rho), tuple(gamma), tuple(c),
            tuple(val[4]), tuple(val[5]), tuple(val[6]),
        )

    none = (jnp.zeros((1, LANES), jnp.float32),) * LR
    one = (jnp.ones((1, LANES), jnp.float32),) * LR
    last = lax.fori_loop(0, ITERS, forward, (one, none, none, none, none, none))
    gamma3, c3, ts, ws, qs = last[1:]

    def adjoint(i, bb, e0, e1, norm_bar, pb, wp, mp, amp):
        ratio = [a / b for a, b in zip(bb, kept(2, i))]
        full = [a + b for a, b in zip(norm_bar, ratio)]
        twice = [2.0 * a for a in full]
        zq, beta = kept(5, i + 1), kept(3, i + 1)
        err = [e0[r] + twice[r] * zq[r] + e1[r] for r in range(LR)]
        put_at(fr, factor_row(me, i + 1, 0), axpy(pb, full, rows(rh, i + 1)))
        put_at(fl, factor_row(me, i + 1, 1), axpy(wp, full, rows(uh, i + 1)))
        factor_send(fr, 0, i + 1, 0)
        factor_send(fl, 1, i + 1, 1)
        rb = axpy([a + b for a, b in zip(rows(rbv, 0), mp)], twice, rows(zh, i + 1))
        put(rbv, 0, rb)
        arb = axpy([a + b for a, b in zip(rows(arbv, 0), amp)], twice, rows(wh, i + 1))
        put(arbv, 0, arb)
        alpha, gamma = kept(0, i), kept(1, i)
        step_bar = [a - b for a, b in zip(kept(4, i), err)]
        curv2 = [-2.0 * (s * a / g) for s, a, g in zip(step_bar, alpha, gamma)]
        norm_bar = [s / g - a * b for s, g, a, b in zip(step_bar, gamma, ratio, beta)]
        diff = [a - b for a, b in zip(rows(tvec, 0), arb)]
        pb = axpy(axpy(scale(beta, pb), alpha, diff), curv2, rows(qh, i + 1))
        put(pbv, 0, pb)
        return tuple(norm_bar)

    alpha3, beta3, zq3 = kept(0, 3), kept(3, 3), kept(5, 3)
    gamma2, c2 = kept(1, 2), kept(4, 2)
    g2 = [-2.0 * (c * a / g) for c, a, g in zip(c3, alpha3, gamma3)]
    mix = lambda a, b: axpy(scale(alpha3, a), g2, b)
    bb = [
        alpha3[r] * c2[r] + g2[r] * (zq3[r] + beta3[r] * gamma2[r]) for r in range(LR)
    ]
    e1 = [alpha3[r] * ts[r] + g2[r] * (ws[r] + beta3[r] * qs[r]) for r in range(LR)]
    norm_bar = adjoint(
        2, bb, none, e1, [c / g for c, g in zip(c3, gamma3)],
        mix(rows(tvec, 0), rows(qh, 4)),
        mix(rows(utv, 0), rows(kv, 0)),
        mix(rows(tmv, 0), rows(sh, 4)),
        mix(rows(atv, 0), rows(yv, 0)),
    )

    def backward(it, norm_bar):
        i = 1 - it
        rd = ITERS + it
        pb = rows(pbv, 0)
        sum_start(
            rd,
            (
                (pb, rows(ph, i + 1)),
                (rows(rbv, 0), rows(qh, i + 1)),
                (pb, rows(sh, i + 1)),
            ),
        )
        precondition(pbv, 0, hvec, 0, 0)
        halo_start(2 + rd, 0)
        sum_middle(rd)
        halo_finish(2 + rd, 0)
        stiffness(0, nvec)
        halo_sent(2 + rd)
        tot = sum_finish(rd)
        bb, e0, e1 = [[tot[r][d : d + 1, :] for r in range(LR)] for d in range(3)]
        return adjoint(
            i, bb, e0, e1, norm_bar,
            rows(pbv, 0), rows(hvec, 0), ext_rows(0), rows(nvec, 0),
        )

    norm_bar = lax.fori_loop(0, 2, backward, norm_bar)

    zeta = factor_row(me, 0, 0)
    put_at(fr, zeta, axpy(rows(pbv, 0), norm_bar, rows(rh, 0)))
    factor_send(fr, 0, 0, 0)
    precondition(fr, zeta, fl, factor_row(me, 0, 1), None)
    factor_send(fl, 1, 0, 1)

    for r in range(LR):
        parts = [xv[pl.ds(r * NBLK + j, 12, stride=4), :] for j in range(4)]
        for i, chunk in enumerate(rows_to_chunks(parts, lane12)):
            sol_ref[pl.ds(2 * i + r, 12, stride=6), :] = chunk

    def factors_wait(j, _):
        for left, buf in ((1, fl), (0, fr)):
            for kind in range(2):
                for d in range(1, nrhs):
                    src = lax.rem(me + d, nrhs)
                    factor_copy(buf, left, j, kind, d, src, src).wait_recv()
                    factor_copy(buf, left, j, kind, d, me, src).wait_send()
        return 0

    lax.fori_loop(0, ITERS, factors_wait, 0)

    depth = nrhs * ITERS * 2 * LR
    lane24 = lax.broadcasted_iota(jnp.int32, (24, LANES), 1)

    def halves(v):
        hi = v.astype(jnp.bfloat16)
        return hi, (v - hi.astype(jnp.float32)).astype(jnp.bfloat16)

    def out_copy(t):
        span = pl.ds(pl.multiple_of(t * CHUNKS * 8, 8), CHUNKS * 8)
        return pltpu.make_async_copy(go.at[span, :], grad_hbm.at[span, :], out_sem.at[t])

    def grads(t, _):
        for s in range(8):
            n = t * 8 + s
            lh, ll = halves(fl[pl.ds(n, depth, stride=NBLK), :])
            rhi, rlo = halves(fr[pl.ds(n, depth, stride=NBLK), :])
            gb[s] = lax.dot_general(
                jnp.concatenate([lh, lh, ll], axis=0),
                jnp.concatenate([rhi, rlo, rhi], axis=0),
                (((0,), (0,)), ((), ())),
                preferred_element_type=jnp.float32,
            )
            parts = [gb[s, pl.ds(j, 24, stride=4), :] for j in range(4)]
            for i, chunk in enumerate(rows_to_chunks(parts, lane24)):
                go[pl.ds(t * (CHUNKS * 8) + i * 8 + s, 24, stride=24), :] = chunk
        out_copy(t).start()
        return 0

    lax.fori_loop(0, TILES, grads, 0)
    for t in range(TILES):
        out_copy(t).wait()


def shards(planes, nrhs, stiffness, precond, rhs_vec, cotangent, col_index, send_rows, counts):
    def flat(v):
        return v.reshape(LR, ROWS // LR, LANES).transpose(1, 0, 2).reshape(ROWS, LANES)

    stiff = stiffness.reshape(NBLK, K, CHUNKS, LANES).transpose(0, 2, 1, 3)
    stiff = stiff.reshape(TILES, 8 * CHUNKS * K, LANES)
    pre = precond.reshape(TILES, 8, CHUNKS, LANES).transpose(0, 2, 1, 3)
    f32 = jnp.float32
    vmem = pl.BlockSpec(memory_space=pltpu.VMEM)
    smem = pl.BlockSpec(memory_space=pltpu.SMEM)
    hbm = pl.BlockSpec(memory_space=pl.ANY)

    def vec(count=1):
        return pltpu.VMEM((count * VEC, LANES), f32)

    dma = pltpu.SemaphoreType.DMA
    factors = nrhs * ITERS * 2 * VEC
    sol, grad = pl.pallas_call(
        functools.partial(kernel, planes, nrhs),
        out_shape=(
            jax.ShapeDtypeStruct((ROWS, LANES), f32),
            jax.ShapeDtypeStruct((TILES * CHUNKS * 8, LANES), f32),
        ),
        in_specs=[smem, smem, smem, vmem, vmem, hbm, hbm],
        out_specs=(vmem, hbm),
        scratch_shapes=[
            pltpu.VMEM((TILES, 8 * CHUNKS * K, LANES), f32),
            pltpu.VMEM((TILES, CHUNKS, K, 8, LANES), f32),
            pltpu.VMEM((TILES, CHUNKS, 8, LANES), f32),
            pltpu.SMEM((NBLK * K,), jnp.int32),
            pltpu.VMEM((2, LR * EXT, LANES), f32),
            vec(K - 1),
        ]
        + [vec() for _ in range(9)]
        + [vec() for _ in range(3)]
        + [vec(ITERS + 1) for _ in range(7)]
        + [
            pltpu.VMEM((LR * 6 * ITERS, LANES), f32),
            pltpu.VMEM((HALOS, 2, LR * 8, LANES), f32),
            pltpu.VMEM((HALOS, 2, LR * 8, LANES), f32),
            pltpu.VMEM((REDS * 8, 8, LANES), f32),
            pltpu.VMEM((REDS * 8, 8, LANES), f32),
            pltpu.VMEM((factors, LANES), f32),
            pltpu.VMEM((factors, LANES), f32),
            pltpu.VMEM((8, LANES, LANES), f32),
            pltpu.VMEM((TILES * CHUNKS * 8, LANES), f32),
            dma((TILES + 1,)),
            dma((TILES,)),
            dma((HALOS, 2)),
            dma((HALOS, 2)),
            dma((REDS * 8,)),
            dma((REDS * 8,)),
            dma((REDS * 8,)),
            dma((REDS * 8,)),
            dma((ITERS * 16,)),
            dma((ITERS * 16,)),
        ],
        compiler_params=pltpu.CompilerParams(
            collective_id=0, has_side_effects=True, vmem_limit_bytes=48 * 1024 * 1024
        ),
        name="cg_adjoint",
    )(col_index, send_rows, counts, flat(rhs_vec), flat(cotangent), stiff, pre)
    sol = sol.reshape(ROWS // LR, LR, LANES).transpose(1, 0, 2).reshape(LR, NBLK * BS)
    grad = grad.reshape(TILES, CHUNKS, 8, LANES).transpose(0, 2, 1, 3)
    return sol, grad.reshape(NBLK, BS * BS)


def solution(mesh):
    in_specs = (
        P("sub", None, None),
        P("sub", None),
        P("rhs", "sub"),
        P("rhs", "sub"),
        P("sub", None),
        P("sub", None),
        P("sub"),
    )
    out_specs = (P("rhs", "sub"), P("sub", None))
    body = functools.partial(shards, mesh.shape["sub"] // PLANE, mesh.shape["rhs"])
    return jax.shard_map(body, mesh=mesh, in_specs=in_specs, out_specs=out_specs, check_vma=False)
```

time: 2000 us -> 124 us (0.06)
  blocking collectives: 1620 us -> 0 us
  matrix products: 170 us -> 0 us
  Pallas kernels: 0 us -> 116 us
  waiting for transfers between devices: 115 us -> 0 us
  starting transfers between devices: 39.2 us -> 0 us
  local copies, waits for them, and re-layouts: 32.9 us -> 6.38 us
    psum x13 -> x0, blocking collectives: 1620 us -> none  [the longest x6 745 us: shards(): lax.psum((local_dot(dir_bar, direction), local_dot(target, direction)), '...]
    dot_general x31 -> x0, matrix products: 170 us -> none  [the longest x8 84.9 us: block_product(): return jnp.einsum('nkab,rnkb->rna', blocks, gathered, precision=highest)]
    pallas_call x0 -> x1, Pallas kernels: none -> 116 us  [shards(): pl.pallas_call(functools.partial(kernel, planes, nrhs), out_shape=(jax.Sh...]
    psum x1 -> x0, waiting for transfers between devices: 106 us -> none  [shards(): grad_sum = lax.psum(grad_sum, 'rhs')]
    ppermute x16 -> x0, starting transfers between devices: 39.2 us -> none  [the longest x8 21.2 us: with_halo(): after = lax.ppermute(initial, axis, down)]
  transfers between devices with their start and end apart: 17 -> 0, of which waited for: 5 -> 0; matrix products, arithmetic and copies ran while one was open for 1% -> 0% of each run, Pallas kernels for 0% -> 0%
where the time goes in v1:
time: 124 us; the launch traced here: 123 us
  Pallas kernels  116 us (94%)
  local copies, waits for them, and re-layouts  6.38 us (5%)
  between operations  1.33 us (1%)
    pallas_call x1, Pallas kernels, shards(): pl.pallas_call(functools.partial(kernel, planes, nrhs), out_shape=(jax.Sh...  116 us
    unnamed x7, local copies, waits for them, and re-layouts  4.74 us

profile of v1, /device:TPU:1, one launch (start us, length us, event | category | flops | bytes accessed | tf_op | source)
XLA Modules:
  0.0 123.3 jit_solution(12664252843066390462)
XLA Ops:
  1.3 0.8 copy.17.col_ref
  2.0 0.8 reshape.37
  2.9 0.8 reshape.39
  3.7 0.0 copy-start
  3.7 1.5 %copy-done = f32[48,9216]{1,0:T(8,128)S(1)} copy-done((f32[48,9216]{1,0:T(8,128)S(1)}, f32[48,9216]{1,0:T(8,128)}, u32[]{:S(2)}) %copy-start) | copy-done | bytes 1769496
  5.2 0.0 copy-start.1
  5.2 0.7 copy-done.1
  5.8 115.6 %cg_adjoint.1 = (f32[72,128]{1,0:T(8,128)S(1)}, f32[3456,128]{1,0:T(8,128)S(1)}) custom-call(s32[48,4]{1,0:T(8,128)S(1)} %copy.17.col_ref, s32[1,12]{1,0:T(1,128)S(1)} %copy-done.1, s32[1]{0:T(128)S(6)} %copy.25.count_ref, f32[72,128]{1,0:T(8,128)S(1)} %bitcast.27, f32[72,128]{1,0:T(8,128)S(1)} %bitcast.28, f32[6,2304,128]{2,1,0:T(8,128)} %bitcast.30, ...), custom_call_target="tpu_custom_call" | custom-call | tf_op jit(solution)/shard_map/cg_adjoint/pallas_call | solution.py:608
  121.5 0.6 copy.23
  122.1 1.2 copy.26
  (3 shorter events, 0.0 us)
Async XLA Ops:
  3.7 1.5 %copy-start = (f32[48,9216]{1,0:T(8,128)S(1)}, f32[48,9216]{1,0:T(8,128)}, u32[]{:S(2)}) copy-start(f32[48,9216]{1,0:T(8,128)} %param.8) | copy-start | bytes 5308420
  5.2 0.7 copy-start.1

commit v2 on v1

--- a/solution.py
+++ b/solution.py
@@ -16,11 +16,10 @@
 LANES = 128
 TILES = NBLK // 8
 CHUNKS = BS * BS // LANES
-GROUPS = CHUNKS // 3
 VEC = LR * NBLK
 ROWS = LR * BS * NBLK // LANES
-PLANE = 8
-UNROLL = 6
+GROUPS = CHUNKS // 3
+SPAN = 24
 HALOS = 8
 REDS = 6
 EXT = 64
@@ -74,97 +73,112 @@
 
 
 def kernel(
-    planes, nrhs,
-    col_ref, send_ref, count_ref, rhs_ref, cot_ref, stiff_hbm, pre_hbm,
-    sol_ref, grad_hbm,
-    raw, blocks, weights, colx, ext, gat, nvec, hvec, tvec, tmv, utv, atv, yv, kv, xv,
-    pbv, rbv, arbv,
-    ph, qh, sh, zh, wh, rh, uh, scr, hsend, hrecv, rb1, rb2, fl, fr, gb, go,
-    load_sem, out_sem, hs_sem, hr_sem, r1s, r1r, r2s, r2r, fs_sem, fr_sem,
+    nsub, nrhs,
+    col_hbm, send_hbm, count_hbm, rhs_ref, cot_ref, stiff_hbm, pre_hbm,
+    sol_ref, go,
+    colx, sendx, countx, flat, blocks, weights, ext, gat,
+    nvec, hvec, tvec, tmv, utv, atv, yv, kv, xv, pbv, rbv, arbv,
+    ph, qh, sh, zh, wh, rh, uh, scr, hsend, hrecv, rbuf, fl, fr, gb,
+    load_sem, small_sem, hs_sem, hr_sem, rs_sem, rr_sem, fs_sem, fr_sem,
 ):
     sub = lax.axis_index("sub")
     me = lax.axis_index("rhs")
-    nsub = planes * PLANE
-    plane = lax.div(sub, PLANE)
-    spot = lax.rem(sub, PLANE)
     lane = lane_iota()
-
-    def in_plane(d):
-        return plane * PLANE + lax.rem(spot + d, PLANE)
-
-    def across(d):
-        return lax.rem(plane + d, planes) * PLANE + spot
-
-    pre_copy = pltpu.make_async_copy(pre_hbm, weights, load_sem.at[TILES])
-    pre_copy.start()
-    stiff_copies = [
-        pltpu.make_async_copy(stiff_hbm.at[t], raw.at[t], load_sem.at[t])
+    f32, bf16 = jnp.float32, jnp.bfloat16
+
+    small = [
+        pltpu.make_async_copy(col_hbm, colx, small_sem.at[0]),
+        pltpu.make_async_copy(send_hbm, sendx, small_sem.at[1]),
+        pltpu.make_async_copy(count_hbm, countx, small_sem.at[2]),
+    ]
+    pre_copies = [
+        pltpu.make_async_copy(
+            pre_hbm.at[t], weights.at[:, pl.ds(8 * t, 8), :], load_sem.at[NBLK + t]
+        )
         for t in range(TILES)
     ]
-    for copy in stiff_copies:
+    for copy in small + pre_copies:
         copy.start()
 
+    def stiff_copy(n):
+        return pltpu.make_async_copy(stiff_hbm.at[n], blocks.at[:, :, n, :], load_sem.at[n])
+
+    for n in range(NBLK):
+        stiff_copy(n).start()
+
     barrier = pltpu.get_barrier_semaphore()
-    peers = 0
-    for d in range(1, PLANE):
-        pl.semaphore_signal(barrier, inc=1, device_id={"sub": in_plane(d)}, device_id_type=MESH)
-        peers += 1
-    for d in range(1, planes):
-        pl.semaphore_signal(barrier, inc=1, device_id={"sub": across(d)}, device_id_type=MESH)
-        peers += 1
+
+    def greet(d, _):
+        pl.semaphore_signal(
+            barrier, inc=1, device_id={"sub": lax.rem(sub + d, nsub)}, device_id_type=MESH
+        )
+        return 0
+
+    lax.fori_loop(1, nsub, greet, 0)
     for d in range(1, nrhs):
-        pl.semaphore_signal(barrier, inc=1, device_id={"rhs": lax.rem(me + d, nrhs)}, device_id_type=MESH)
-        peers += 1
+        pl.semaphore_signal(
+            barrier, inc=1, device_id={"rhs": lax.rem(me + d, nrhs)}, device_id_type=MESH
+        )
+    peers = nsub - 1 + nrhs - 1
     before = lax.rem(sub + nsub - 1, nsub)
     after = lax.rem(sub + 1, nsub)
-    for other in (before, after):
-        pl.semaphore_signal(barrier, inc=1, device_id={"sub": other}, device_id_type=MESH)
-        peers += 1
-
+
+    hsend[...] = jnp.zeros_like(hsend)
+    for ref in (ph, qh, sh):
+        ref[pl.ds(0, VEC), :] = jnp.zeros((VEC, LANES), f32)
+    for ref in (yv, kv, xv, rbv, arbv):
+        ref[...] = jnp.zeros_like(ref)
+    for copy in small:
+        copy.wait()
     for n in range(NBLK):
         for k in range(1, K):
-            c = col_ref[n, k]
-            colx[n * K + k] = jnp.where(
+            c = colx[k, n]
+            colx[k, n] = jnp.where(
                 c < IF, c + NBLK, jnp.where(c < IF + NBLK, c - IF, c + 8 - IF)
             )
-    hsend[...] = jnp.zeros_like(hsend)
-    for ref in (ph, qh, sh):
-        ref[pl.ds(0, VEC), :] = jnp.zeros((VEC, LANES), jnp.float32)
-    for ref in (yv, kv, xv, rbv, arbv):
-        ref[...] = jnp.zeros_like(ref)
 
     lane12 = lax.broadcasted_iota(jnp.int32, (12, LANES), 1)
     row12 = lax.broadcasted_iota(jnp.int32, (12, LANES), 0)
-    live = count_ref[0]
+    live = countx[0]
+    for c in range(ROWS // LR):
+        flat[0, pl.ds(LR * c, LR), :] = rhs_ref[:, pl.ds(c * LANES, LANES)]
+        flat[1, pl.ds(LR * c, LR), :] = cot_ref[:, pl.ds(c * LANES, LANES)]
     for r in range(LR):
-        chunks = [rhs_ref[pl.ds(2 * i + r, 12, stride=6), :] for i in range(3)]
+        chunks = [flat[0, pl.ds(2 * i + r, 12, stride=6), :] for i in range(3)]
         for j, row in enumerate(chunks_to_rows(chunks, lane12)):
             row = jnp.where(row12 * 4 + j < live, row, jnp.zeros_like(row))
             rh[pl.ds(r * NBLK + j, 12, stride=4), :] = row
-        chunks = [cot_ref[pl.ds(2 * i + r, 12, stride=6), :] for i in range(3)]
+        chunks = [flat[1, pl.ds(2 * i + r, 12, stride=6), :] for i in range(3)]
         for j, row in enumerate(chunks_to_rows(chunks, lane12)):
             tvec[pl.ds(r * NBLK + j, 12, stride=4), :] = row
 
+    def halves(v):
+        hi = v.astype(bf16)
+        return hi, (v - hi.astype(f32)).astype(bf16)
+
+    def row_sums(v):
+        return [
+            jnp.broadcast_to(jnp.sum(p, axis=1, keepdims=True), (8, LANES))
+            for p in row_parts(v, lane)
+        ]
+
     def precondition(src, base, dst, dst_base, slot):
         full = slot is not None
 
         def tile(t, _):
+            at = pl.multiple_of(8 * t, 8)
             x = [src[pl.ds(pl.multiple_of(base + r * NBLK + 8 * t, 8), 8), :] for r in range(LR)]
             pat = [patterns(v, lane) for v in x]
-            zero = jnp.zeros((8, LANES), jnp.float32)
+            zero = jnp.zeros((8, LANES), f32)
 
             def step(s, carry):
                 proj, acc = carry
                 proj, acc = list(proj), [list(a) for a in acc]
-                for q in range(UNROLL):
-                    g = s * UNROLL + q
-                    w = [weights[t, 3 * g + i] for i in range(3)]
+                for q in range(SPAN):
+                    g = s * SPAN + q
+                    w = [weights[3 * g + i, pl.ds(at, 8), :] for i in range(3)]
                     for r in range(LR):
-                        parts = row_parts([w[i] * pat[r][i] for i in range(3)], lane)
-                        sums = [
-                            jnp.broadcast_to(jnp.sum(p, axis=1, keepdims=True), (8, LANES))
-                            for p in parts
-                        ]
+                        sums = row_sums([w[i] * pat[r][i] for i in range(3)])
                         for j in range(4):
                             proj[r] = jnp.where(lane == 4 * g + j, sums[j], proj[r])
                         if full:
@@ -173,8 +187,11 @@
                             acc[r][2] += w[2] * jnp.where(lane < 32, sums[2], sums[3])
                 return tuple(proj), tuple(tuple(a) for a in acc)
 
-            start = ((zero,) * LR, ((zero,) * 3,) * LR)
-            proj, acc = lax.fori_loop(0, GROUPS // UNROLL, step, start)
+            carry = ((zero,) * LR, ((zero,) * 3,) * LR)
+            if SPAN == GROUPS:
+                proj, acc = step(0, carry)
+            else:
+                proj, acc = lax.fori_loop(0, GROUPS // SPAN, step, carry)
             for r in range(LR):
                 dst[pl.ds(pl.multiple_of(dst_base + r * NBLK + 8 * t, 8), 8), :] = proj[r]
                 if full:
@@ -209,7 +226,7 @@
     def halo_start(h, slot):
         for side in range(2):
             for j in range(IF):
-                idx = send_ref[0, side * IF + j]
+                idx = sendx[0, side * IF + j]
                 for r in range(LR):
                     hsend[h, side, pl.ds(r * 8 + j, 1), :] = ext[slot, pl.ds(r * EXT + idx, 1), :]
         for copy in halo_copies(h):
@@ -236,7 +253,7 @@
             for q in range(4):
                 n = s * 4 + q
                 for k in range(1, K):
-                    c = colx[n * K + k]
+                    c = colx[k, n]
                     for r in range(LR):
                         gat[pl.ds(((k - 1) * LR + r) * NBLK + n, 1), :] = ext[
                             slot, pl.ds(r * EXT + c, 1), :
@@ -246,6 +263,7 @@
         lax.fori_loop(0, NBLK // 4, gather, 0)
 
         def tile(t, _):
+            at = pl.multiple_of(8 * t, 8)
             pat = []
             for r in range(LR):
                 own = ext[slot, pl.ds(pl.multiple_of(r * EXT + 8 * t, 8), 8), :]
@@ -254,85 +272,79 @@
                     for k in range(1, K)
                 ]
                 pat.append([patterns(v, lane) for v in [own] + rest])
-            zero = jnp.zeros((8, LANES), jnp.float32)
 
             def step(s, out):
                 out = list(out)
-                for q in range(UNROLL):
-                    g = s * UNROLL + q
+                for q in range(SPAN):
+                    g = s * SPAN + q
                     prod = [[None] * 3 for _ in range(LR)]
                     for i in range(3):
-                        a = [blocks[t, 3 * g + i, k] for k in range(K)]
+                        a = [blocks[3 * g + i, k, pl.ds(at, 8), :] for k in range(K)]
                         for r in range(LR):
                             prod[r][i] = (a[0] * pat[r][0][i] + a[1] * pat[r][1][i]) + (
                                 a[2] * pat[r][2][i] + a[3] * pat[r][3][i]
                             )
                     for r in range(LR):
-                        for j, p in enumerate(row_parts(prod[r], lane)):
-                            s_j = jnp.broadcast_to(jnp.sum(p, axis=1, keepdims=True), (8, LANES))
-                            out[r] = jnp.where(lane == 4 * g + j, s_j, out[r])
+                        for j, v in enumerate(row_sums(prod[r])):
+                            out[r] = jnp.where(lane == 4 * g + j, v, out[r])
                 return tuple(out)
 
-            out = lax.fori_loop(0, GROUPS // UNROLL, step, (zero,) * LR)
+            out = (jnp.zeros((8, LANES), f32),) * LR
+            if SPAN == GROUPS:
+                out = step(0, out)
+            else:
+                out = lax.fori_loop(0, GROUPS // SPAN, step, out)
             for r in range(LR):
                 dst[pl.ds(pl.multiple_of(r * NBLK + 8 * t, 8), 8), :] = out[r]
             return 0
 
         lax.fori_loop(0, TILES, tile, 0)
 
-    def stage_copy(buf, ssem, rsem, rd, d, mine, target):
-        at = rd * 8 + mine
+    def sum_copy(rd, d):
+        at = rd * nsub + sub
         return pltpu.make_async_remote_copy(
-            src_ref=buf.at[at], dst_ref=buf.at[at],
-            send_sem=ssem.at[rd * 8 + d], recv_sem=rsem.at[at],
-            device_id={"sub": target}, device_id_type=MESH,
-        )
-
-    def arrived(buf, ssem, rsem, rd, d, source, target):
-        at = rd * 8 + source
-        pltpu.make_async_remote_copy(
-            src_ref=buf.at[at], dst_ref=buf.at[at],
-            send_sem=ssem.at[rd * 8 + d], recv_sem=rsem.at[at],
-            device_id={"sub": target}, device_id_type=MESH,
-        ).wait_recv()
+            src_ref=rbuf.at[at], dst_ref=rbuf.at[at],
+            send_sem=rs_sem.at[rd], recv_sem=rr_sem.at[rd],
+            device_id={"sub": lax.rem(sub + d, nsub)}, device_id_type=MESH,
+        )
+
+    srow = lax.broadcasted_iota(jnp.int32, (8, LANES), 0)
 
     def sum_start(rd, pairs):
-        tiles = []
-        srow = lax.broadcasted_iota(jnp.int32, (8, LANES), 0)
+        payload = jnp.zeros((8, LANES), f32)
         for r in range(LR):
-            tile = jnp.zeros((8, LANES), jnp.float32)
+            tile = jnp.zeros((8, LANES), f32)
             for d, (a, b) in enumerate(pairs):
                 row = jnp.sum(a[r] * b[r], axis=0, keepdims=True)
                 tile = jnp.where(srow == d, jnp.broadcast_to(row, (8, LANES)), tile)
-            tiles.append(jnp.sum(tile, axis=1, keepdims=True))
-        rb1[rd * 8 + spot] = jnp.where(
-            lane < 64,
-            jnp.broadcast_to(tiles[0], (8, LANES)),
-            jnp.broadcast_to(tiles[1], (8, LANES)),
-        )
-        for d in range(1, PLANE):
-            stage_copy(rb1, r1s, r1r, rd, d, spot, in_plane(d)).start()
-
-    def sum_middle(rd):
-        for d in range(1, PLANE):
-            arrived(rb1, r1s, r1r, rd, d, lax.rem(spot + d, PLANE), in_plane(d))
-        v = [rb1[rd * 8 + s] for s in range(PLANE)]
-        rb2[rd * 8 + plane] = ((v[0] + v[1]) + (v[2] + v[3])) + ((v[4] + v[5]) + (v[6] + v[7]))
-        for d in range(1, planes):
-            stage_copy(rb2, r2s, r2r, rd, d, plane, across(d)).start()
+            tot = jnp.broadcast_to(jnp.sum(tile, axis=1, keepdims=True), (8, LANES))
+            payload = jnp.where(lane == srow + 64 * r, tot, payload)
+        rbuf[rd * nsub + sub] = jnp.sum(payload, axis=0, keepdims=True)
+
+        def send(d, _):
+            sum_copy(rd, d).start()
+            return 0
+
+        lax.fori_loop(1, nsub, send, 0)
 
     def sum_finish(rd):
-        for d in range(1, planes):
-            arrived(rb2, r2s, r2r, rd, d, lax.rem(plane + d, planes), across(d))
-        v = rb2[rd * 8]
-        for s in range(1, planes):
-            v = v + rb2[rd * 8 + s]
-        swapped = pltpu.roll(v, 64, 1)
-        for d in range(1, PLANE):
-            stage_copy(rb1, r1s, r1r, rd, d, spot, in_plane(d)).wait_send()
-        for d in range(1, planes):
-            stage_copy(rb2, r2s, r2r, rd, d, plane, across(d)).wait_send()
-        return (jnp.where(lane < 64, v, swapped), jnp.where(lane < 64, swapped, v))
+        span = rbuf.at[pl.ds(rd * nsub, nsub - 1)]
+        pltpu.make_async_copy(span, span, rr_sem.at[rd]).wait()
+        parts = [jnp.zeros((1, LANES), f32)] * 4
+        for s in range(nsub):
+            parts[s % 4] = parts[s % 4] + rbuf[rd * nsub + s]
+        row = jnp.broadcast_to((parts[0] + parts[1]) + (parts[2] + parts[3]), (8, LANES))
+        pltpu.make_async_copy(span, span, rs_sem.at[rd]).wait()
+        return [
+            jnp.broadcast_to(
+                jnp.sum(
+                    jnp.where(lane == srow + 64 * r, row, jnp.zeros_like(row)),
+                    axis=1, keepdims=True,
+                ),
+                (8, LANES),
+            )
+            for r in range(LR)
+        ]
 
     def factor_row(src, j, kind):
         return pl.multiple_of(((src * ITERS + j) * 2 + kind) * VEC, 8)
@@ -379,7 +391,8 @@
     def kept(kind, i):
         return [scr[pl.ds((r * 6 + kind) * ITERS + i, 1), :] for r in range(LR)]
 
-    pre_copy.wait()
+    for copy in pre_copies:
+        copy.wait()
     precondition(rh, 0, uh, 0, 0)
     pl.semaphore_wait(barrier, peers)
     halo_start(0, 0)
@@ -387,17 +400,8 @@
     precondition(tvec, 0, utv, 0, 1)
     halo_start(1, 1)
     put(tmv, 0, ext_rows(1))
-    for t in range(TILES):
-        stiff_copies[t].wait()
-
-        def relay(s, _, t=t):
-            for q in range(4):
-                c = s * 4 + q
-                for k in range(K):
-                    blocks[t, c, k] = raw[t, pl.ds(c * K + k, 8, stride=CHUNKS * K), :]
-            return 0
-
-        lax.fori_loop(0, CHUNKS // 4, relay, 0)
+    for n in range(NBLK):
+        stiff_copy(n).wait()
     halo_finish(0, 0)
     stiffness(0, nvec)
     put(wh, 0, rows(nvec, 0))
@@ -425,7 +429,6 @@
         put_at(fr, at, rows(rh, i))
         factor_send(fl, 1, i, 0)
         factor_send(fr, 0, i, 1)
-        sum_middle(i)
         halo_finish(2 + i, 0)
         stiffness(0, nvec)
         halo_sent(2 + i)
@@ -520,7 +523,6 @@
         )
         precondition(pbv, 0, hvec, 0, 0)
         halo_start(2 + rd, 0)
-        sum_middle(rd)
         halo_finish(2 + rd, 0)
         stiffness(0, nvec)
         halo_sent(2 + rd)
@@ -542,7 +544,9 @@
     for r in range(LR):
         parts = [xv[pl.ds(r * NBLK + j, 12, stride=4), :] for j in range(4)]
         for i, chunk in enumerate(rows_to_chunks(parts, lane12)):
-            sol_ref[pl.ds(2 * i + r, 12, stride=6), :] = chunk
+            flat[0, pl.ds(2 * i + r, 12, stride=6), :] = chunk
+    for c in range(ROWS // LR):
+        sol_ref[:, pl.ds(c * LANES, LANES)] = flat[0, pl.ds(LR * c, LR), :]
 
     def factors_wait(j, _):
         for left, buf in ((1, fl), (0, fr)):
@@ -557,14 +561,6 @@
 
     depth = nrhs * ITERS * 2 * LR
     lane24 = lax.broadcasted_iota(jnp.int32, (24, LANES), 1)
-
-    def halves(v):
-        hi = v.astype(jnp.bfloat16)
-        return hi, (v - hi.astype(jnp.float32)).astype(jnp.bfloat16)
-
-    def out_copy(t):
-        span = pl.ds(pl.multiple_of(t * CHUNKS * 8, 8), CHUNKS * 8)
-        return pltpu.make_async_copy(go.at[span, :], grad_hbm.at[span, :], out_sem.at[t])
 
     def grads(t, _):
         for s in range(8):
@@ -580,25 +576,17 @@
             parts = [gb[s, pl.ds(j, 24, stride=4), :] for j in range(4)]
             for i, chunk in enumerate(rows_to_chunks(parts, lane24)):
                 go[pl.ds(t * (CHUNKS * 8) + i * 8 + s, 24, stride=24), :] = chunk
-        out_copy(t).start()
         return 0
 
     lax.fori_loop(0, TILES, grads, 0)
-    for t in range(TILES):
-        out_copy(t).wait()
-
-
-def shards(planes, nrhs, stiffness, precond, rhs_vec, cotangent, col_index, send_rows, counts):
-    def flat(v):
-        return v.reshape(LR, ROWS // LR, LANES).transpose(1, 0, 2).reshape(ROWS, LANES)
-
+
+
+def shards(nsub, nrhs, stiffness, precond, rhs_vec, cotangent, col_index, send_rows, counts):
     stiff = stiffness.reshape(NBLK, K, CHUNKS, LANES).transpose(0, 2, 1, 3)
-    stiff = stiff.reshape(TILES, 8 * CHUNKS * K, LANES)
     pre = precond.reshape(TILES, 8, CHUNKS, LANES).transpose(0, 2, 1, 3)
     f32 = jnp.float32
     vmem = pl.BlockSpec(memory_space=pltpu.VMEM)
-    smem = pl.BlockSpec(memory_space=pltpu.SMEM)
-    hbm = pl.BlockSpec(memory_space=pl.ANY)
+    hbm = pl.BlockSpec(memory_space=pltpu.HBM)
 
     def vec(count=1):
         return pltpu.VMEM((count * VEC, LANES), f32)
@@ -606,42 +594,39 @@
     dma = pltpu.SemaphoreType.DMA
     factors = nrhs * ITERS * 2 * VEC
     sol, grad = pl.pallas_call(
-        functools.partial(kernel, planes, nrhs),
+        functools.partial(kernel, nsub, nrhs),
         out_shape=(
-            jax.ShapeDtypeStruct((ROWS, LANES), f32),
+            jax.ShapeDtypeStruct((LR, NBLK * BS), f32),
             jax.ShapeDtypeStruct((TILES * CHUNKS * 8, LANES), f32),
         ),
-        in_specs=[smem, smem, smem, vmem, vmem, hbm, hbm],
-        out_specs=(vmem, hbm),
+        in_specs=[hbm, hbm, hbm, vmem, vmem, hbm, hbm],
+        out_specs=(vmem, vmem),
         scratch_shapes=[
-            pltpu.VMEM((TILES, 8 * CHUNKS * K, LANES), f32),
-            pltpu.VMEM((TILES, CHUNKS, K, 8, LANES), f32),
-            pltpu.VMEM((TILES, CHUNKS, 8, LANES), f32),
-            pltpu.SMEM((NBLK * K,), jnp.int32),
+            pltpu.SMEM((K, NBLK), jnp.int32),
+            pltpu.SMEM((1, 2 * IF), jnp.int32),
+            pltpu.SMEM((1,), jnp.int32),
+            pltpu.VMEM((2, ROWS, LANES), f32),
+            pltpu.VMEM((CHUNKS, K, NBLK, LANES), f32),
+            pltpu.VMEM((CHUNKS, NBLK, LANES), f32),
             pltpu.VMEM((2, LR * EXT, LANES), f32),
             vec(K - 1),
         ]
-        + [vec() for _ in range(9)]
-        + [vec() for _ in range(3)]
+        + [vec() for _ in range(12)]
         + [vec(ITERS + 1) for _ in range(7)]
         + [
             pltpu.VMEM((LR * 6 * ITERS, LANES), f32),
             pltpu.VMEM((HALOS, 2, LR * 8, LANES), f32),
             pltpu.VMEM((HALOS, 2, LR * 8, LANES), f32),
-            pltpu.VMEM((REDS * 8, 8, LANES), f32),
-            pltpu.VMEM((REDS * 8, 8, LANES), f32),
+            pltpu.VMEM((REDS * nsub, 1, LANES), f32),
             pltpu.VMEM((factors, LANES), f32),
             pltpu.VMEM((factors, LANES), f32),
             pltpu.VMEM((8, LANES, LANES), f32),
-            pltpu.VMEM((TILES * CHUNKS * 8, LANES), f32),
-            dma((TILES + 1,)),
-            dma((TILES,)),
+            dma((NBLK + TILES,)),
+            dma((3,)),
             dma((HALOS, 2)),
             dma((HALOS, 2)),
-            dma((REDS * 8,)),
-            dma((REDS * 8,)),
-            dma((REDS * 8,)),
-            dma((REDS * 8,)),
+            dma((REDS,)),
+            dma((REDS,)),
             dma((ITERS * 16,)),
             dma((ITERS * 16,)),
         ],
@@ -649,8 +634,7 @@
             collective_id=0, has_side_effects=True, vmem_limit_bytes=48 * 1024 * 1024
         ),
         name="cg_adjoint",
-    )(col_index, send_rows, counts, flat(rhs_vec), flat(cotangent), stiff, pre)
-    sol = sol.reshape(ROWS // LR, LR, LANES).transpose(1, 0, 2).reshape(LR, NBLK * BS)
+    )(col_index.T, send_rows, counts, rhs_vec, cotangent, stiff, pre)
     grad = grad.reshape(TILES, CHUNKS, 8, LANES).transpose(0, 2, 1, 3)
     return sol, grad.reshape(NBLK, BS * BS)
 
@@ -666,5 +650,5 @@
         P("sub"),
     )
     out_specs = (P("rhs", "sub"), P("sub", None))
-    body = functools.partial(shards, mesh.shape["sub"] // PLANE, mesh.shape["rhs"])
+    body = functools.partial(shards, mesh.shape["sub"], mesh.shape["rhs"])
     return jax.shard_map(body, mesh=mesh, in_specs=in_specs, out_specs=out_specs, check_vma=False)

time: 124 us -> 102 us (0.82)
  Pallas kernels: 116 us -> 94.5 us
    pallas_call x1, Pallas kernels: 116 us -> 94.5 us  [shards(): pl.pallas_call(functools.partial(kernel, nsub, nrhs), out_shape=(jax.Shap...]
    reshape x3 -> x0, local copies, waits for them, and re-layouts: 1.6 us -> none  [the longest x2 1.6 us: flat(): v.reshape(LR, ROWS // LR, LANES).transpose(1, 0, 2).reshape(ROWS, LANES)]
    unnamed x7 -> x12, local copies, waits for them, and re-layouts: 4.74 us -> 6.17 us
where the time goes in v2:
time: 102 us
  Pallas kernels  94.5 us (93%)
  local copies, waits for them, and re-layouts  6.17 us (6%)
  between operations  1.3 us (1%)
    pallas_call x1, Pallas kernels, shards(): pl.pallas_call(functools.partial(kernel, nsub, nrhs), out_shape=(jax.Shap...  94.5 us
    unnamed x12, local copies, waits for them, and re-layouts  6.17 us

profile of v2, /device:TPU:1, one launch (start us, length us, event | category | flops | bytes accessed | tf_op | source)
XLA Modules:
  0.0 102.0 jit_solution(5482140850534746569)
XLA Ops:
  1.3 0.0 copy-start
  1.3 1.5 %copy-done = f32[48,9216]{1,0:T(8,128)S(1)} copy-done((f32[48,9216]{1,0:T(8,128)S(1)}, f32[48,9216]{1,0:T(8,128)}, u32[]{:S(2)}) %copy-start) | copy-done | bytes 1769496
  2.8 0.0 copy-start.1
  2.8 0.8 copy-done.1
  3.5 0.0 copy-start.2
  3.5 0.8 copy-done.2
  4.3 0.0 copy-start.3
  4.3 0.7 copy-done.3
  5.0 0.0 copy-start.4
  5.0 0.7 copy-done.4
  5.6 94.5 %cg_adjoint.1 = (f32[2,4608]{1,0:T(2,128)S(1)}, f32[3456,128]{1,0:T(8,128)S(1)}) custom-call(s32[4,48]{1,0:T(4,128)S(1)} %bitcast.14, s32[1,12]{1,0:T(1,128)S(1)} %copy-done.4, s32[1]{0:T(128)S(6)} %copy.11.count_hbm, f32[2,4608]{1,0:T(2,128)S(1)} %copy-done.1, f32[2,4608]{1,0:T(2,128)S(1)} %copy-done.2, f32[48,72,4,128]{3,2,1,0:T(4,128)} %bitcast.15, ...), custom_call_target="tpu_custom_call" | custom-call | tf_op jit(solution)/shard_map/cg_adjoint/pallas_call | solution.py:596
  100.2 0.6 copy.12
  100.8 1.2 %copy.13 = f32[48,9216]{1,0:T(8,128)} copy(f32[48,9216]{1,0:T(8,128)S(1)} %bitcast.12) | data formatting | bytes 3538944
Async XLA Ops:
  1.3 1.5 %copy-start = (f32[48,9216]{1,0:T(8,128)S(1)}, f32[48,9216]{1,0:T(8,128)}, u32[]{:S(2)}) copy-start(f32[48,9216]{1,0:T(8,128)} %param.8) | copy-start | bytes 5308420
  2.8 0.8 copy-start.1
  3.5 0.8 copy-start.2
  4.3 0.7 copy-start.3
  5.0 0.7 copy-start.4

commit v3 on v2

--- a/solution.py
+++ b/solution.py
@@ -19,10 +19,10 @@
 VEC = LR * NBLK
 ROWS = LR * BS * NBLK // LANES
 GROUPS = CHUNKS // 3
-SPAN = 24
 HALOS = 8
 REDS = 6
-EXT = 64
+EXT = 56
+RIM = 24
 MESH = pl.DeviceIdType.MESH
 
 
@@ -76,7 +76,7 @@
     nsub, nrhs,
     col_hbm, send_hbm, count_hbm, rhs_ref, cot_ref, stiff_hbm, pre_hbm,
     sol_ref, go,
-    colx, sendx, countx, flat, blocks, weights, ext, gat,
+    colx, rimx, sendx, countx, flat, blocks, faces, weights, ext, gat, rim, rimg,
     nvec, hvec, tvec, tmv, utv, atv, yv, kv, xv, pbv, rbv, arbv,
     ph, qh, sh, zh, wh, rh, uh, scr, hsend, hrecv, rbuf, fl, fr, gb,
     load_sem, small_sem, hs_sem, hr_sem, rs_sem, rr_sem, fs_sem, fr_sem,
@@ -130,12 +130,25 @@
         ref[...] = jnp.zeros_like(ref)
     for copy in small:
         copy.wait()
+    for q in range(2 * IF):
+        for k in range(1, K):
+            c = colx[k, sendx[0, q]]
+            rimx[k, q] = jnp.where(
+                c < IF, c, jnp.where(c < IF + NBLK, 16, c + 8 - IF - NBLK)
+            )
     for n in range(NBLK):
         for k in range(1, K):
-            c = colx[k, n]
-            colx[k, n] = jnp.where(
-                c < IF, c + NBLK, jnp.where(c < IF + NBLK, c - IF, c + 8 - IF)
-            )
+            c = colx[k, n] - IF
+            colx[k, n] = jnp.where((c >= 0) & (c < NBLK), c, NBLK)
+    ext[...] = jnp.zeros_like(ext)
+    rim[...] = jnp.zeros_like(rim)
+    rimg[...] = jnp.zeros_like(rimg)
+
+    def clear(c, _):
+        faces[c] = jnp.zeros((K - 1, 16, LANES), f32)
+        return 0
+
+    lax.fori_loop(0, CHUNKS, clear, 0)
 
     lane12 = lax.broadcasted_iota(jnp.int32, (12, LANES), 1)
     row12 = lax.broadcasted_iota(jnp.int32, (12, LANES), 0)
@@ -162,52 +175,52 @@
             for p in row_parts(v, lane)
         ]
 
-    def precondition(src, base, dst, dst_base, slot):
+    def precondition(src, base, dst, dst_base, slot, rd=None):
         full = slot is not None
 
-        def tile(t, _):
-            at = pl.multiple_of(8 * t, 8)
-            x = [src[pl.ds(pl.multiple_of(base + r * NBLK + 8 * t, 8), 8), :] for r in range(LR)]
-            pat = [patterns(v, lane) for v in x]
+        def pair(s, _):
+            if rd is not None:
+                for q in range((nsub - 1) // 3):
+                    sum_copy(rd, s * ((nsub - 1) // 3) + q).start()
+            tiles = (2 * s, 2 * s + 1)
+            at = [pl.multiple_of(8 * t, 8) for t in tiles]
+            items = [(b, r) for b in range(2) for r in range(LR)]
+            x = {
+                (b, r): src[pl.ds(pl.multiple_of(base + r * NBLK + at[b], 8), 8), :]
+                for b, r in items
+            }
+            pat = {m: patterns(x[m], lane) for m in items}
             zero = jnp.zeros((8, LANES), f32)
-
-            def step(s, carry):
-                proj, acc = carry
-                proj, acc = list(proj), [list(a) for a in acc]
-                for q in range(SPAN):
-                    g = s * SPAN + q
-                    w = [weights[3 * g + i, pl.ds(at, 8), :] for i in range(3)]
+            proj = {m: zero for m in items}
+            acc = {m: [zero] * 3 for m in items}
+            for g in range(GROUPS):
+                for b in range(2):
+                    w = [weights[3 * g + i, pl.ds(at[b], 8), :] for i in range(3)]
                     for r in range(LR):
-                        sums = row_sums([w[i] * pat[r][i] for i in range(3)])
+                        m = (b, r)
+                        sums = row_sums([w[i] * pat[m][i] for i in range(3)])
                         for j in range(4):
-                            proj[r] = jnp.where(lane == 4 * g + j, sums[j], proj[r])
+                            proj[m] = jnp.where(lane == 4 * g + j, sums[j], proj[m])
                         if full:
-                            acc[r][0] += w[0] * jnp.where(lane < 96, sums[0], sums[1])
-                            acc[r][1] += w[1] * jnp.where(lane < 64, sums[1], sums[2])
-                            acc[r][2] += w[2] * jnp.where(lane < 32, sums[2], sums[3])
-                return tuple(proj), tuple(tuple(a) for a in acc)
-
-            carry = ((zero,) * LR, ((zero,) * 3,) * LR)
-            if SPAN == GROUPS:
-                proj, acc = step(0, carry)
-            else:
-                proj, acc = lax.fori_loop(0, GROUPS // SPAN, step, carry)
-            for r in range(LR):
-                dst[pl.ds(pl.multiple_of(dst_base + r * NBLK + 8 * t, 8), 8), :] = proj[r]
+                            acc[m][0] += w[0] * jnp.where(lane < 96, sums[0], sums[1])
+                            acc[m][1] += w[1] * jnp.where(lane < 64, sums[1], sums[2])
+                            acc[m][2] += w[2] * jnp.where(lane < 32, sums[2], sums[3])
+            for b, r in items:
+                dst[pl.ds(pl.multiple_of(dst_base + r * NBLK + at[b], 8), 8), :] = proj[b, r]
                 if full:
-                    a = acc[r]
+                    a = acc[b, r]
                     total = (
                         a[0]
                         + pltpu.roll(jnp.where(lane >= 96, a[0], a[1]), 32, 1)
                         + pltpu.roll(jnp.where(lane >= 64, a[1], a[2]), 64, 1)
                         + pltpu.roll(a[2], 96, 1)
                     )
-                    ext[slot, pl.ds(pl.multiple_of(r * EXT + 8 * t, 8), 8), :] = x[r] + jnp.where(
-                        lane < 96, total, zero
-                    )
+                    ext[slot, pl.ds(pl.multiple_of(r * EXT + at[b], 8), 8), :] = x[
+                        b, r
+                    ] + jnp.where(lane < 96, total, zero)
             return 0
 
-        lax.fori_loop(0, TILES, tile, 0)
+        lax.fori_loop(0, TILES // 2, pair, 0)
 
     def halo_copies(h):
         return (
@@ -232,7 +245,7 @@
         for copy in halo_copies(h):
             copy.start()
 
-    def halo_finish(h, slot):
+    def halo_finish(h, dst):
         for copy in halo_copies(h):
             copy.wait_recv()
         for side in range(2):
@@ -240,9 +253,44 @@
             inside = jnp.broadcast_to(edge, (8, LANES)) > 0
             for r in range(LR):
                 v = hrecv[h, side, pl.ds(r * 8, 8), :]
-                ext[slot, pl.ds(r * EXT + NBLK + 8 * side, 8), :] = jnp.where(
-                    inside, v, jnp.zeros_like(v)
-                )
+                rim[pl.ds(r * RIM + 8 * side, 8), :] = jnp.where(inside, v, jnp.zeros_like(v))
+        for q in range(2 * IF):
+            for k in range(1, K):
+                c = rimx[k, q]
+                for r in range(LR):
+                    rimg[pl.ds(((k - 1) * LR + r) * 16 + q, 1), :] = rim[pl.ds(r * RIM + c, 1), :]
+        out = {}
+        for t in range(2):
+            pat = [
+                [
+                    patterns(rimg[pl.ds(((k - 1) * LR + r) * 16 + 8 * t, 8), :], lane)
+                    for k in range(1, K)
+                ]
+                for r in range(LR)
+            ]
+            acc = [jnp.zeros((8, LANES), f32)] * LR
+            for g in range(GROUPS):
+                prod = [[None] * 3 for _ in range(LR)]
+                for i in range(3):
+                    a = [faces[3 * g + i, k, pl.ds(8 * t, 8), :] for k in range(K - 1)]
+                    for r in range(LR):
+                        prod[r][i] = (a[0] * pat[r][0][i] + a[1] * pat[r][1][i]) + (
+                            a[2] * pat[r][2][i]
+                        )
+                for r in range(LR):
+                    for j, v in enumerate(row_sums(prod[r])):
+                        acc[r] = jnp.where(lane == 4 * g + j, v, acc[r])
+            for r in range(LR):
+                out[t, r] = acc[r]
+        block = lax.broadcasted_iota(jnp.int32, (NBLK, LANES), 0)
+        total = [dst[pl.ds(r * NBLK, NBLK), :] for r in range(LR)]
+        for q in range(2 * IF):
+            hit = block == sendx[0, q]
+            for r in range(LR):
+                row = jnp.broadcast_to(out[q // 8, r][q % 8 : q % 8 + 1], (NBLK, LANES))
+                total[r] = total[r] + jnp.where(hit, row, jnp.zeros_like(row))
+        for r in range(LR):
+            dst[pl.ds(r * NBLK, NBLK), :] = total[r]
 
     def halo_sent(h):
         for copy in halo_copies(h):
@@ -273,34 +321,26 @@
                 ]
                 pat.append([patterns(v, lane) for v in [own] + rest])
 
-            def step(s, out):
-                out = list(out)
-                for q in range(SPAN):
-                    g = s * SPAN + q
-                    prod = [[None] * 3 for _ in range(LR)]
-                    for i in range(3):
-                        a = [blocks[3 * g + i, k, pl.ds(at, 8), :] for k in range(K)]
-                        for r in range(LR):
-                            prod[r][i] = (a[0] * pat[r][0][i] + a[1] * pat[r][1][i]) + (
-                                a[2] * pat[r][2][i] + a[3] * pat[r][3][i]
-                            )
+            out = [jnp.zeros((8, LANES), f32)] * LR
+            for g in range(GROUPS):
+                prod = [[None] * 3 for _ in range(LR)]
+                for i in range(3):
+                    a = [blocks[3 * g + i, k, pl.ds(at, 8), :] for k in range(K)]
                     for r in range(LR):
-                        for j, v in enumerate(row_sums(prod[r])):
-                            out[r] = jnp.where(lane == 4 * g + j, v, out[r])
-                return tuple(out)
-
-            out = (jnp.zeros((8, LANES), f32),) * LR
-            if SPAN == GROUPS:
-                out = step(0, out)
-            else:
-                out = lax.fori_loop(0, GROUPS // SPAN, step, out)
+                        prod[r][i] = (a[0] * pat[r][0][i] + a[1] * pat[r][1][i]) + (
+                            a[2] * pat[r][2][i] + a[3] * pat[r][3][i]
+                        )
+                for r in range(LR):
+                    for j, v in enumerate(row_sums(prod[r])):
+                        out[r] = jnp.where(lane == 4 * g + j, v, out[r])
             for r in range(LR):
                 dst[pl.ds(pl.multiple_of(r * NBLK + 8 * t, 8), 8), :] = out[r]
             return 0
 
         lax.fori_loop(0, TILES, tile, 0)
 
-    def sum_copy(rd, d):
+    def sum_copy(rd, m):
+        d = nsub // 2 + lax.div(m + 1, 2) * (2 * lax.rem(m, 2) - 1)
         at = rd * nsub + sub
         return pltpu.make_async_remote_copy(
             src_ref=rbuf.at[at], dst_ref=rbuf.at[at],
@@ -310,7 +350,7 @@
 
     srow = lax.broadcasted_iota(jnp.int32, (8, LANES), 0)
 
-    def sum_start(rd, pairs):
+    def sum_local(rd, pairs):
         payload = jnp.zeros((8, LANES), f32)
         for r in range(LR):
             tile = jnp.zeros((8, LANES), f32)
@@ -320,12 +360,6 @@
             tot = jnp.broadcast_to(jnp.sum(tile, axis=1, keepdims=True), (8, LANES))
             payload = jnp.where(lane == srow + 64 * r, tot, payload)
         rbuf[rd * nsub + sub] = jnp.sum(payload, axis=0, keepdims=True)
-
-        def send(d, _):
-            sum_copy(rd, d).start()
-            return 0
-
-        lax.fori_loop(1, nsub, send, 0)
 
     def sum_finish(rd):
         span = rbuf.at[pl.ds(rd * nsub, nsub - 1)]
@@ -402,11 +436,19 @@
     put(tmv, 0, ext_rows(1))
     for n in range(NBLK):
         stiff_copy(n).wait()
-    halo_finish(0, 0)
+
+    def face(c, _):
+        for k in range(1, K):
+            for q in range(2 * IF):
+                faces[c, k - 1, pl.ds(q, 1), :] = blocks[c, k, pl.ds(sendx[0, q], 1), :]
+        return 0
+
+    lax.fori_loop(0, CHUNKS, face, 0)
     stiffness(0, nvec)
+    halo_finish(0, nvec)
     put(wh, 0, rows(nvec, 0))
-    halo_finish(1, 1)
     stiffness(1, atv)
+    halo_finish(1, atv)
     halo_sent(0)
     halo_sent(1)
 
@@ -414,14 +456,14 @@
         rho_old, gamma_old, c_old = carry[:3]
         z, w, res, t = rows(zh, i), rows(wh, i), rows(rh, i), rows(tvec, 0)
         q_old, s_old = rows(qh, i), rows(sh, i)
-        sum_start(
+        sum_local(
             i,
             (
                 (res, z), (z, w), (z, q_old), (t, z),
                 (t, s_old), (w, s_old), (q_old, s_old),
             ),
         )
-        precondition(wh, i * VEC, hvec, 0, 0)
+        precondition(wh, i * VEC, hvec, 0, 0, i)
         halo_start(2 + i, 0)
         at = factor_row(me, i, 0)
         put_at(fl, at, rows(uh, i))
@@ -429,8 +471,8 @@
         put_at(fr, at, rows(rh, i))
         factor_send(fl, 1, i, 0)
         factor_send(fr, 0, i, 1)
-        halo_finish(2 + i, 0)
         stiffness(0, nvec)
+        halo_finish(2 + i, nvec)
         halo_sent(2 + i)
         tot = sum_finish(i)
         val = [[tot[r][d : d + 1, :] for r in range(LR)] for d in range(7)]
@@ -513,7 +555,7 @@
         i = 1 - it
         rd = ITERS + it
         pb = rows(pbv, 0)
-        sum_start(
+        sum_local(
             rd,
             (
                 (pb, rows(ph, i + 1)),
@@ -521,10 +563,10 @@
                 (pb, rows(sh, i + 1)),
             ),
         )
-        precondition(pbv, 0, hvec, 0, 0)
+        precondition(pbv, 0, hvec, 0, 0, rd)
         halo_start(2 + rd, 0)
-        halo_finish(2 + rd, 0)
         stiffness(0, nvec)
+        halo_finish(2 + rd, nvec)
         halo_sent(2 + rd)
         tot = sum_finish(rd)
         bb, e0, e1 = [[tot[r][d : d + 1, :] for r in range(LR)] for d in range(3)]
@@ -603,13 +645,17 @@
         out_specs=(vmem, vmem),
         scratch_shapes=[
             pltpu.SMEM((K, NBLK), jnp.int32),
+            pltpu.SMEM((K, 2 * IF), jnp.int32),
             pltpu.SMEM((1, 2 * IF), jnp.int32),
             pltpu.SMEM((1,), jnp.int32),
             pltpu.VMEM((2, ROWS, LANES), f32),
             pltpu.VMEM((CHUNKS, K, NBLK, LANES), f32),
+            pltpu.VMEM((CHUNKS, K - 1, 16, LANES), f32),
             pltpu.VMEM((CHUNKS, NBLK, LANES), f32),
             pltpu.VMEM((2, LR * EXT, LANES), f32),
             vec(K - 1),
+            pltpu.VMEM((LR * RIM, LANES), f32),
+            pltpu.VMEM(((K - 1) * LR * 16, LANES), f32),
         ]
         + [vec() for _ in range(12)]
         + [vec(ITERS + 1) for _ in range(7)]
@@ -631,7 +677,7 @@
             dma((ITERS * 16,)),
         ],
         compiler_params=pltpu.CompilerParams(
-            collective_id=0, has_side_effects=True, vmem_limit_bytes=48 * 1024 * 1024
+            collective_id=0, has_side_effects=True, vmem_limit_bytes=62 * 1024 * 1024
         ),
         name="cg_adjoint",
     )(col_index.T, send_rows, counts, rhs_vec, cotangent, stiff, pre)

time: 102 us -> 89 us (0.87); the launches traced: 102 us -> 87.9 us
  Pallas kernels: 94.5 us -> 82.4 us
  local copies, waits for them, and re-layouts: 6.17 us -> 4.18 us
    pallas_call x1, Pallas kernels: 94.5 us -> 82.4 us  [shards(): pl.pallas_call(functools.partial(kernel, nsub, nrhs), out_shape=(jax.Shap...]
    unnamed x12 -> x2, local copies, waits for them, and re-layouts: 6.17 us -> 4.18 us
where the time goes in v3:
time: 89 us; the launch traced here: 87.9 us
  Pallas kernels  82.4 us (93%)
  local copies, waits for them, and re-layouts  4.18 us (5%)
  between operations  1.29 us (1%)
    pallas_call x1, Pallas kernels, shards(): pl.pallas_call(functools.partial(kernel, nsub, nrhs), out_shape=(jax.Shap...  82.4 us
    unnamed x2, local copies, waits for them, and re-layouts  4.18 us

profile of v3, /device:TPU:1, one launch (start us, length us, event | category | flops | bytes accessed | tf_op | source)
XLA Modules:
  0.0 87.9 jit_solution(2147090893029899179)
XLA Ops:
  1.3 82.4 %cg_adjoint.1 = (f32[2,4608]{1,0:T(2,128)}, f32[3456,128]{1,0:T(8,128)}) custom-call(s32[4,48]{1,0:T(4,128)} %bitcast.15, s32[1,12]{1,0:T(1,128)} %send_hbm.1, s32[1]{0:T(128)S(6)} %copy.11.count_hbm, f32[2,4608]{1,0:T(2,128)} %rhs_ref.1, f32[2,4608]{1,0:T(2,128)} %cot_ref.1, f32[48,72,4,128]{3,2,1,0:T(4,128)} %bitcast.12, f32[6,72,8,128]{3,2,1,0:T(8,128)} %bitcast.14), custom_call_target="tpu_custom_call" | custom-call | tf_op jit(solution)/shard_map/cg_adjoint/pallas_call | solution.py:638
  83.7 1.4 %copy.12 = f32[2,4608]{1,0:T(2,128)} copy(f32[2,4608]{1,0:T(2,128)} %get-tuple-element.8) | data formatting | bytes 73728
  85.1 2.8 %copy.13 = f32[48,9216]{1,0:T(8,128)} copy(f32[48,9216]{1,0:T(8,128)} %bitcast.13) | data formatting | bytes 3538944

commit v4 on v3

--- a/solution.py
+++ b/solution.py
@@ -78,8 +78,8 @@
     sol_ref, go,
     colx, rimx, sendx, countx, flat, blocks, faces, weights, ext, gat, rim, rimg,
     nvec, hvec, tvec, tmv, utv, atv, yv, kv, xv, pbv, rbv, arbv,
-    ph, qh, sh, zh, wh, rh, uh, scr, hsend, hrecv, rbuf, fl, fr, gb,
-    load_sem, small_sem, hs_sem, hr_sem, rs_sem, rr_sem, fs_sem, fr_sem,
+    ph, qh, sh, zh, wh, rh, uh, scr, hsend, hrecv, rbuf, fl, fr, nf, gb,
+    load_sem, small_sem, hs_sem, hr_sem, rs_sem, rr_sem, fs_sem, fr_sem, ns_sem, nr_sem,
 ):
     sub = lax.axis_index("sub")
     me = lax.axis_index("rhs")
@@ -396,6 +396,14 @@
         for d in range(1, nrhs):
             factor_copy(buf, left, j, kind, d, me, lax.rem(me + d, nrhs)).start()
 
+    def weight_copy(it, d, src, target):
+        at = src * 2 + it
+        return pltpu.make_async_remote_copy(
+            src_ref=nf.at[at], dst_ref=nf.at[at],
+            send_sem=ns_sem.at[it * 4 + d], recv_sem=nr_sem.at[at],
+            device_id={"rhs": target}, device_id_type=MESH,
+        )
+
     def rows(ref, i):
         return [
             ref[pl.ds(pl.multiple_of(i * VEC + r * NBLK, 8), NBLK), :] for r in range(LR)
@@ -512,16 +520,22 @@
     last = lax.fori_loop(0, ITERS, forward, (one, none, none, none, none, none))
     gamma3, c3, ts, ws, qs = last[1:]
 
-    def adjoint(i, bb, e0, e1, norm_bar, pb, wp, mp, amp):
+    def adjoint(i, bb, e0, e1, norm_bar, pb, wp, mp, amp, it=None):
         ratio = [a / b for a, b in zip(bb, kept(2, i))]
         full = [a + b for a, b in zip(norm_bar, ratio)]
         twice = [2.0 * a for a in full]
         zq, beta = kept(5, i + 1), kept(3, i + 1)
         err = [e0[r] + twice[r] * zq[r] + e1[r] for r in range(LR)]
-        put_at(fr, factor_row(me, i + 1, 0), axpy(pb, full, rows(rh, i + 1)))
-        put_at(fl, factor_row(me, i + 1, 1), axpy(wp, full, rows(uh, i + 1)))
-        factor_send(fr, 0, i + 1, 0)
-        factor_send(fl, 1, i + 1, 1)
+        if it is None:
+            put_at(fr, factor_row(me, i + 1, 0), axpy(pb, full, rows(rh, i + 1)))
+            put_at(fl, factor_row(me, i + 1, 1), axpy(wp, full, rows(uh, i + 1)))
+            factor_send(fr, 0, i + 1, 0)
+            factor_send(fl, 1, i + 1, 1)
+        else:
+            tile = [jnp.broadcast_to(a, (8, LANES)) for a in full]
+            nf[me * 2 + it] = jnp.where(srow == 0, tile[0], tile[1])
+            for d in range(1, nrhs):
+                weight_copy(it, d, me, lax.rem(me + d, nrhs)).start()
         rb = axpy([a + b for a, b in zip(rows(rbv, 0), mp)], twice, rows(zh, i + 1))
         put(rbv, 0, rb)
         arb = axpy([a + b for a, b in zip(rows(arbv, 0), amp)], twice, rows(wh, i + 1))
@@ -565,6 +579,10 @@
         )
         precondition(pbv, 0, hvec, 0, 0, rd)
         halo_start(2 + rd, 0)
+        put_at(fr, factor_row(me, i + 1, 0), rows(pbv, 0))
+        factor_send(fr, 0, i + 1, 0)
+        put_at(fl, factor_row(me, i + 1, 1), rows(hvec, 0))
+        factor_send(fl, 1, i + 1, 1)
         stiffness(0, nvec)
         halo_finish(2 + rd, nvec)
         halo_sent(2 + rd)
@@ -572,7 +590,7 @@
         bb, e0, e1 = [[tot[r][d : d + 1, :] for r in range(LR)] for d in range(3)]
         return adjoint(
             i, bb, e0, e1, norm_bar,
-            rows(pbv, 0), rows(hvec, 0), ext_rows(0), rows(nvec, 0),
+            rows(pbv, 0), rows(hvec, 0), ext_rows(0), rows(nvec, 0), it,
         )
 
     norm_bar = lax.fori_loop(0, 2, backward, norm_bar)
@@ -600,6 +618,25 @@
         return 0
 
     lax.fori_loop(0, ITERS, factors_wait, 0)
+    for it in range(2):
+        for d in range(1, nrhs):
+            src = lax.rem(me + d, nrhs)
+            weight_copy(it, d, src, src).wait_recv()
+            weight_copy(it, d, me, src).wait_send()
+
+    def finish(src, _):
+        for it in range(2):
+            j = 2 - it
+            weight = nf[src * 2 + it]
+            for buf, kind in ((fr, 0), (fl, 1)):
+                at, other = factor_row(src, j, kind), factor_row(src, j, 1 - kind)
+                for r in range(LR):
+                    here = pl.ds(pl.multiple_of(at + r * NBLK, 8), NBLK)
+                    there = pl.ds(pl.multiple_of(other + r * NBLK, 8), NBLK)
+                    buf[here, :] = buf[here, :] + weight[r : r + 1] * buf[there, :]
+        return 0
+
+    lax.fori_loop(0, nrhs, finish, 0)
 
     depth = nrhs * ITERS * 2 * LR
     lane24 = lax.broadcasted_iota(jnp.int32, (24, LANES), 1)
@@ -666,6 +703,7 @@
             pltpu.VMEM((REDS * nsub, 1, LANES), f32),
             pltpu.VMEM((factors, LANES), f32),
             pltpu.VMEM((factors, LANES), f32),
+            pltpu.VMEM((nrhs * 2, 8, LANES), f32),
             pltpu.VMEM((8, LANES, LANES), f32),
             dma((NBLK + TILES,)),
             dma((3,)),
@@ -675,6 +713,8 @@
             dma((REDS,)),
             dma((ITERS * 16,)),
             dma((ITERS * 16,)),
+            dma((8,)),
+            dma((nrhs * 2,)),
         ],
         compiler_params=pltpu.CompilerParams(
             collective_id=0, has_side_effects=True, vmem_limit_bytes=62 * 1024 * 1024

time: 89 us -> 85.4 us (0.960); the launches traced: 87.9 us -> 85.2 us
  Pallas kernels: 82.4 us -> 79.7 us
    pallas_call x1, Pallas kernels: 82.4 us -> 79.7 us  [shards(): pl.pallas_call(functools.partial(kernel, nsub, nrhs), out_shape=(jax.Shap...]
where the time goes in v4:
time: 85.4 us; the launch traced here: 85.2 us
  Pallas kernels  79.7 us (93%)
  local copies, waits for them, and re-layouts  4.18 us (5%)
  between operations  1.29 us (2%)
    pallas_call x1, Pallas kernels, shards(): pl.pallas_call(functools.partial(kernel, nsub, nrhs), out_shape=(jax.Shap...  79.7 us
    unnamed x2, local copies, waits for them, and re-layouts  4.18 us

profile of v4, /device:TPU:1, one launch (start us, length us, event | category | flops | bytes accessed | tf_op | source)
XLA Modules:
  0.0 85.2 jit_solution(16296237810100600076)
XLA Ops:
  1.3 79.7 %cg_adjoint.1 = (f32[2,4608]{1,0:T(2,128)}, f32[3456,128]{1,0:T(8,128)}) custom-call(s32[4,48]{1,0:T(4,128)} %bitcast.15, s32[1,12]{1,0:T(1,128)} %send_hbm.1, s32[1]{0:T(128)S(6)} %copy.11.count_hbm, f32[2,4608]{1,0:T(2,128)} %rhs_ref.1, f32[2,4608]{1,0:T(2,128)} %cot_ref.1, f32[48,72,4,128]{3,2,1,0:T(4,128)} %bitcast.12, f32[6,72,8,128]{3,2,1,0:T(8,128)} %bitcast.14), custom_call_target="tpu_custom_call" | custom-call | tf_op jit(solution)/shard_map/cg_adjoint/pallas_call | solution.py:675
  81.0 1.4 %copy.12 = f32[2,4608]{1,0:T(2,128)} copy(f32[2,4608]{1,0:T(2,128)} %get-tuple-element.8) | data formatting | bytes 73728
  82.4 2.8 %copy.13 = f32[48,9216]{1,0:T(8,128)} copy(f32[48,9216]{1,0:T(8,128)} %bitcast.13) | data formatting | bytes 3538944
